TPU v7x, 128 devices: a whole 4x4x4 slice. The times are simulated.
128 devices in a mesh: tensor: 2 (over core), req: 16 (over x, z), seq: 4 (over y).
Axes of the slice: x: 4, y: 4, z: 4, core: 2. Of those that a mesh axis runs over, the one named last changes fastest.
Arguments:
- incoming_activations: bfloat16 [32, 1024, 4096], P('req', 'seq'), may hold values from -6 to 6
- standardize_scaling: float32 [4096], replicated, may hold values from 0.1 to 1.9
- lagged_blending_weights: float32 [4, 4096], replicated, may hold values from 0 to 1
- learner_line_permutation: int32 [4096], replicated, may hold values from 0 to 4095, each once
- learner_acceptor_lookup_slices: float32 [3, 4096, 2048], P(None, ('req', 'seq'), 'tensor'), may hold values from -0.09375 to 0.09375
- learner_projection_slices: float32 [2048, 4096], P('tensor', ('req', 'seq')), may hold values from -0.125 to 0.125
- fading_left_matrix: bfloat16 [4096, 128], replicated, may hold values from -0.09375 to 0.09375
- fading_right_matrix: bfloat16 [128, 2048], P(None, 'tensor'), may hold values from -0.5 to 0.5
- feature_fading_speed: float32 [2048], P('tensor'), may hold values from 0.0002 to 0.08
- self_reward: float32 [2048], P('tensor'), may hold values from -3 to 3
- cluster_scaling_vector: float32 [2048], P('tensor'), may hold values from 0.1 to 1.9
- prompt_extents: int32 [32], P('req'), may hold values from 128 to 1024, as said below
Outputs:
- hidden_out: bfloat16 [32, 1024, 4096], P('req', 'seq', 'tensor')
- stretch_states: float32 [32, 4, 32, 4096], P('req', 'seq', 'tensor')
Inputs may be any that keep to these rules, and one draw needn't show every extreme that they name: `prompt_extents`: it counts the valid tokens of each prompt from its start; prompt 0 is always full. learner_line_permutation names each of the 4096 input rows once.
All inputs are finite; a program needn't handle non-finite values.
Results may differ from a plain program's by a relative error of at most 0.013.
Values may be sent and summed in bfloat16 or wider, within the bound.
A program may use at most 192 MiB of HBM per device.

v0:
```python
import functools

import jax
import jax.numpy as jnp
from jax import lax
from jax.experimental import pallas as pl
from jax.experimental.pallas import tpu as pltpu
from jax.sharding import PartitionSpec as P

ATTEND_DIM = 64
PAIR = 128
CHUNK = 128
COLS = 256
SAFE = -60.0
eps = 1e-05
f32 = jnp.float32
bf16 = jnp.bfloat16
HIGHEST = lax.Precision.HIGHEST
CONTRACT_ROWS = (((0,), (0,)), ((), ()))
CONTRACT_LANES = (((1,), (1,)), ((), ()))


def from_behind(value, axis, by):
    peers = lax.axis_size(axis)
    pairs = [(i, i + by) for i in range(peers) if 0 <= i + by < peers]
    return lax.ppermute(value, axis, pairs)


def split_two(value):
    high = value.astype(bf16)
    low = (value - high.astype(f32)).astype(bf16)
    return high, low


def dot32(a, b, dims=(((1,), (0,)), ((), ()))):
    return lax.dot_general(a, b, dims, preferred_element_type=f32)


def mix_kernel(
    x_ref, tail_ref, perm_ref, gain_ref, blend_ref, left_ref, mr_ref, mk_ref, mv_ref, lora_ref,
    stack, chosen, stats, low_rank,
):
    rows, width = x_ref.shape
    span = rows // tail_ref.shape[0]
    step = pl.program_id(0)

    @pl.when(step == 0)
    def _():
        stack[:rows, :] = x_ref[...]
        table = jnp.concatenate([gain_ref[...], blend_ref[0:3, :]], axis=0)
        first = table.astype(bf16)
        rest = table - first.astype(f32)
        second = rest.astype(bf16)
        third = (rest - second.astype(f32)).astype(bf16)
        pad = jnp.zeros((2, width), bf16)
        stack[rows:, :] = jnp.concatenate([tail_ref[...], first, second, third, pad], axis=0)
        low_rank[...] = jnp.zeros_like(low_rank)

        def row_stats(i, _):
            at = pl.ds(pl.multiple_of(i * 16, 16), 16)
            part = stack[at, :].astype(f32)
            mean = jnp.mean(part, axis=-1, keepdims=True)
            centred = part - mean
            spread = jnp.mean(centred * centred, axis=-1, keepdims=True)
            stats[0, at, :] = jnp.broadcast_to(mean, (16, PAIR))
            stats[1, at, :] = jnp.broadcast_to(lax.rsqrt(spread + eps), (16, PAIR))
            return 0

        lax.fori_loop(0, stack.shape[0] // 16, row_stats, 0)

    mean, scale = stats[0, :, 0:1], stats[1, :, 0:1]
    row = lax.broadcasted_iota(jnp.int32, (rows, 1), 0)

    def shifted(values, gain):
        normal = (values - mean[: values.shape[0]]) * scale[: values.shape[0]] * gain
        current = normal[:rows]
        previous = pltpu.roll(current, 1, axis=0)
        for b in range(rows // span):
            previous = jnp.where(row == b * span, normal[rows + b : rows + b + 1], previous)
        return current, previous - current

    names = perm_ref[...]

    def one_hot(i, _):
        base = pl.multiple_of(i * COLS, COLS)
        feature = lax.broadcasted_iota(jnp.int32, (COLS, COLS), 0) + base
        chosen[pl.ds(base, COLS), :] = (feature == names).astype(f32).astype(bf16)
        return 0

    lax.fori_loop(0, width // COLS, one_hot, 0)
    picked = dot32(stack[...], chosen[...])
    table = picked[rows + 2 : rows + 6] + picked[rows + 6 : rows + 10] + picked[rows + 10 : rows + 14]
    current, delta = shifted(picked, table[0:1])
    mr_ref[...] = (current + delta * table[1:2]).astype(bf16)
    mk_ref[...] = (current + delta * table[2:3]).astype(bf16)
    mv_ref[...] = (current + delta * table[3:4]).astype(bf16)

    here = pl.ds(pl.multiple_of(step * COLS, COLS), COLS)
    current, delta = shifted(stack[:, here].astype(f32), gain_ref[:, here])
    mixed = (current + delta * blend_ref[3:4, here]).astype(bf16)
    low_rank[...] += dot32(mixed, left_ref[...])

    @pl.when(step == pl.num_programs(0) - 1)
    def _():
        lora_ref[...] = jnp.tanh(low_rank[...]).astype(bf16)


def mix(x, tail, perm, gain, blend, left):
    rows, width = x.shape
    whole = lambda shape: pl.BlockSpec(shape, lambda i: (0,) * len(shape))
    column = pl.BlockSpec((rows, COLS), lambda i: (0, i))
    out = jax.ShapeDtypeStruct((rows, width), bf16)
    return pl.pallas_call(
        mix_kernel,
        grid=(width // COLS,),
        in_specs=[
            whole((rows, width)),
            whole(tail.shape),
            pl.BlockSpec((1, COLS), lambda i: (0, i)),
            whole((1, width)),
            whole((4, width)),
            pl.BlockSpec((COLS, left.shape[1]), lambda i: (i, 0)),
        ],
        out_specs=[column, column, column, whole((rows, left.shape[1]))],
        out_shape=[out, out, out, jax.ShapeDtypeStruct((rows, left.shape[1]), bf16)],
        scratch_shapes=[
            pltpu.VMEM((rows + 16, width), bf16),
            pltpu.VMEM((width, COLS), bf16),
            pltpu.VMEM((2, rows + 16, PAIR), f32),
            pltpu.VMEM((rows, left.shape[1]), f32),
        ],
        compiler_params=pltpu.CompilerParams(vmem_limit_bytes=48 << 20),
        cost_estimate=pl.CostEstimate(
            flops=2 * rows * width * width, bytes_accessed=16 * rows * width, transcendentals=0
        ),
        name="mix",
    )(x, tail, perm, gain, blend, left)


def earlier(size):
    t = lax.broadcasted_iota(jnp.int32, (size, size), 0)
    s = lax.broadcasted_iota(jnp.int32, (size, size), 1)
    return t > s


def same_head():
    c = lax.broadcasted_iota(jnp.int32, (PAIR, PAIR), 0) // ATTEND_DIM
    v = lax.broadcasted_iota(jnp.int32, (PAIR, PAIR), 1) // ATTEND_DIM
    return c == v


def sum_before(decays):
    ones = earlier(decays.shape[0]).astype(f32).astype(bf16)
    high, low = split_two(decays)
    return dot32(ones, high) + dot32(ones, low)


def sum_after(decays):
    ones = earlier(decays.shape[0]).astype(f32).astype(bf16)
    high, low = split_two(decays)
    return dot32(ones, high, CONTRACT_ROWS) + dot32(ones, low, CONTRACT_ROWS)


def column_total(decays):
    high, low = split_two(decays)
    ones = jnp.ones((decays.shape[0], PAIR), bf16)
    return dot32(high, ones, CONTRACT_ROWS) + dot32(low, ones, CONTRACT_ROWS)


def state_kernel(span, valid_ref, lora_ref, right_ref, speed_ref, k_ref, v_ref, w_ref, l_ref, t_ref):
    rows = k_ref.shape[0]
    valid = valid_ref[:, 0:1]
    log_decay = -speed_ref[...] * jnp.exp(dot32(lora_ref[...], right_ref[...])) * valid
    w_ref[...] = log_decay
    keep = same_head()
    for b in range(rows // span):
        at = slice(b * span, (b + 1) * span)
        part = log_decay[at]
        left_over = jnp.exp(sum_after(part))
        key = (k_ref[at].astype(f32) * valid[at] * left_over).astype(bf16)
        state = dot32(key, v_ref[at], CONTRACT_ROWS)
        l_ref[b, 0] = jnp.where(keep, state, 0.0).astype(l_ref.dtype)
        t_ref[b, 0] = column_total(part)


def local_states(valid, lora, right, speed, k, v, span):
    rows, width = k.shape
    pairs, reqs = width // PAIR, rows // span
    column = pl.BlockSpec((rows, PAIR), lambda i: (0, i))
    whole = lambda shape: pl.BlockSpec(shape, lambda i: (0,) * len(shape))
    piece = pl.BlockSpec((reqs, 1, PAIR, PAIR), lambda i: (0, i, 0, 0))
    return pl.pallas_call(
        functools.partial(state_kernel, span),
        grid=(pairs,),
        in_specs=[
            whole(valid.shape), whole(lora.shape),
            pl.BlockSpec((right.shape[0], PAIR), lambda i: (0, i)),
            pl.BlockSpec((1, PAIR), lambda i: (0, i)),
            column, column,
        ],
        out_specs=[column, piece, piece],
        out_shape=[
            jax.ShapeDtypeStruct((rows, width), f32),
            jax.ShapeDtypeStruct((reqs, pairs, PAIR, PAIR), bf16),
            jax.ShapeDtypeStruct((reqs, pairs, PAIR, PAIR), f32),
        ],
        compiler_params=pltpu.CompilerParams(vmem_limit_bytes=32 << 20),
        cost_estimate=pl.CostEstimate(flops=10**9, bytes_accessed=8 << 20, transcendentals=10**6),
        name="local_states",
    )(valid, lora, right, speed, k, v)


def within_chunk_stepwise(r, k, v, w):
    rows = lax.broadcasted_iota(jnp.int32, (CHUNK, 1), 0)
    ones = jnp.ones((CHUNK, PAIR), f32)
    keep = same_head()

    def token(t, carried):
        state, out = carried
        mine = rows == t
        dot = functools.partial(lax.dot_general, precision=HIGHEST, preferred_element_type=f32)
        out = out + dot(jnp.where(mine, r, 0.0), state, (((1,), (0,)), ((), ())))
        fade = jnp.exp(dot(jnp.where(mine, w, 0.0), ones, CONTRACT_ROWS))
        dyad = jnp.where(keep, dot(jnp.where(mine, k, 0.0), v, CONTRACT_ROWS), 0.0)
        return fade * state + dyad, out

    zero = jnp.zeros((PAIR, PAIR), f32)
    return lax.fori_loop(0, CHUNK, token, (zero, jnp.zeros((CHUNK, PAIR), f32)))[1]


def read_kernel(
    span, valid_ref, r_ref, k_ref, v_ref, w_ref, in_ref, l_ref, t_ref, reward_ref, scale_ref,
    out_ref, state_ref, inner,
):
    rows = k_ref.shape[0]
    keep = same_head()
    average = jnp.where(keep, 1.0, 0.0).astype(bf16)
    first_head = lax.broadcasted_iota(jnp.int32, (1, PAIR), 1) < ATTEND_DIM
    strict = earlier(CHUNK)
    strict = jnp.concatenate([strict, strict], axis=1)
    for b in range(rows // span):
        state = in_ref[b, 0]
        final = jnp.exp(t_ref[b, 0]) * state + l_ref[b, 0].astype(f32)
        state_ref[b, 0, 0] = final[:ATTEND_DIM, :ATTEND_DIM]
        state_ref[b, 0, 1] = final[ATTEND_DIM:, ATTEND_DIM:]
        for c in range(span // CHUNK):
            at = slice(b * span + c * CHUNK, b * span + (c + 1) * CHUNK)
            valid = valid_ref[at, 0:1]
            r, v = r_ref[at].astype(f32), v_ref[at]
            k = k_ref[at].astype(f32) * valid
            w = w_ref[at]
            before = sum_before(w)
            cum = before + w
            mid, last = before[CHUNK // 2 : CHUNK // 2 + 1], cum[CHUNK - 1 :]
            gentle = jnp.min(jnp.minimum(mid, last - mid)) > SAFE

            @pl.when(gentle)
            def _():
                query = (r * jnp.exp(before - mid)).astype(bf16)
                key = k * jnp.exp(mid - cum)
                keys = jnp.concatenate(
                    [jnp.where(first_head, key, 0.0), jnp.where(first_head, 0.0, key)], axis=0
                ).astype(bf16)
                scores = jnp.where(strict, dot32(query, keys, CONTRACT_LANES), 0.0).astype(bf16)
                value = v.astype(f32)
                values = jnp.concatenate(
                    [jnp.where(first_head, value, 0.0), jnp.where(first_head, 0.0, value)], axis=0
                ).astype(bf16)
                inner[...] = dot32(scores, values)

            @pl.when(jnp.logical_not(gentle))
            def _():
                inner[...] = within_chunk_stepwise(r, k, v.astype(f32), w)

            high, low = split_two(r * reward_ref[...] * k)
            own = (dot32(high, average) + dot32(low, average)) * v.astype(f32)
            y = inner[...] + own + dot32((r * jnp.exp(before)).astype(bf16), state.astype(bf16))
            if c + 1 < span // CHUNK:
                left_over = (k * jnp.exp(sum_after(w))).astype(bf16)
                grown = dot32(left_over, v, CONTRACT_ROWS)
                state = jnp.exp(column_total(w)) * state + jnp.where(keep, grown, 0.0)
            high, low = split_two(y)
            centred = y - (dot32(high, average) + dot32(low, average)) * (1.0 / ATTEND_DIM)
            high, low = split_two(centred * centred)
            spread = (dot32(high, average) + dot32(low, average)) * (1.0 / ATTEND_DIM)
            normed = centred * lax.rsqrt(spread + eps) * scale_ref[...] * valid
            out_ref[at] = normed.astype(bf16)


def read_states(valid, r, k, v, w, incoming, local_state, totals, reward, scale, span):
    rows, width = k.shape
    pairs, reqs = width // PAIR, rows // span
    column = pl.BlockSpec((rows, PAIR), lambda i: (0, i))
    line = pl.BlockSpec((1, PAIR), lambda i: (0, i))
    piece = pl.BlockSpec((reqs, 1, PAIR, PAIR), lambda i: (0, i, 0, 0))
    heads = pl.BlockSpec((reqs, 1, 2, ATTEND_DIM, ATTEND_DIM), lambda i: (0, i, 0, 0, 0))
    return pl.pallas_call(
        functools.partial(read_kernel, span),
        grid=(pairs,),
        in_specs=[
            pl.BlockSpec(valid.shape, lambda i: (0, 0)),
            column, column, column, column, piece, piece, piece, line, line,
        ],
        out_specs=[column, heads],
        out_shape=[
            jax.ShapeDtypeStruct((rows, width), bf16),
            jax.ShapeDtypeStruct((reqs, pairs, 2, ATTEND_DIM, ATTEND_DIM), f32),
        ],
        scratch_shapes=[pltpu.VMEM((CHUNK, PAIR), f32)],
        compiler_params=pltpu.CompilerParams(vmem_limit_bytes=32 << 20),
        cost_estimate=pl.CostEstimate(flops=2 * 10**9, bytes_accessed=8 << 20, transcendentals=10**6),
        name="read_states",
    )(valid, r, k, v, w, incoming, local_state, totals, reward, scale)


def local(
    incoming_activations,
    standardize_scaling,
    lagged_blending_weights,
    learner_line_permutation,
    learner_acceptor_lookup_slices,
    learner_projection_slices,
    fading_left_matrix,
    fading_right_matrix,
    feature_fading_speed,
    self_reward,
    cluster_scaling_vector,
    prompt_extents,
):
    reqs, span, width = incoming_activations.shape
    rows = reqs * span
    local_width = feature_fading_speed.shape[0]
    pairs = local_width // PAIR
    x = incoming_activations.reshape(rows, width)
    weights = learner_acceptor_lookup_slices.astype(bf16)
    gather = functools.partial(lax.all_gather, axis_name=("req", "seq"), tiled=True)
    weight_k = gather(weights[1], axis=0)
    weight_v = gather(weights[2], axis=0)
    weight_r = gather(weights[0], axis=0)
    weight_out = gather(learner_projection_slices.T.astype(bf16), axis=0)
    tail = from_behind(incoming_activations[:, span - 1, :], "seq", 1)
    positions = lax.axis_index("seq") * span + jnp.arange(span, dtype=jnp.int32)
    valid = (positions[None, :] < prompt_extents[:, None]).astype(f32).reshape(rows, 1)
    valid = jnp.broadcast_to(valid, (rows, PAIR))
    mixed_r, mixed_k, mixed_v, lora = mix(
        x, tail, learner_line_permutation[None], standardize_scaling[None],
        lagged_blending_weights, fading_left_matrix,
    )
    k = dot32(mixed_k, weight_k).astype(bf16)
    v = dot32(mixed_v, weight_v).astype(bf16)
    decays, states, totals = local_states(
        valid, lora, fading_right_matrix, feature_fading_speed[None], k, v, span
    )
    incoming = jnp.zeros(states.shape, f32)
    sent = jnp.zeros_like(totals)
    for by in range(1, lax.axis_size("seq")):
        far_state = from_behind(states, "seq", by).astype(f32)
        incoming = incoming + jnp.exp(sent) * far_state
        if by + 1 < lax.axis_size("seq"):
            far_total = from_behind(totals[..., 0], "seq", by)
            sent = sent + far_total[..., None]
    r = dot32(mixed_r, weight_r).astype(bf16)
    normed, final = read_states(
        valid, r, k, v, decays, incoming, states, totals,
        self_reward[None], cluster_scaling_vector[None], span,
    )
    stretch_states = final.reshape(reqs, 1, local_width // ATTEND_DIM, ATTEND_DIM * ATTEND_DIM)
    terms = dot32(normed, weight_out, CONTRACT_LANES)
    summed = lax.psum_scatter(
        terms.astype(bf16), "tensor", scatter_dimension=1, tiled=True
    ).astype(f32)
    share = width // lax.axis_size("tensor")
    residual = lax.dynamic_slice_in_dim(x, lax.axis_index("tensor") * share, share, 1)
    hidden_out = (residual.astype(f32) + summed).astype(bf16).reshape(reqs, span, share)
    return (hidden_out, stretch_states)


def solution(mesh):
    in_specs = (
        P("req", "seq", None),
        P(),
        P(),
        P(),
        P(None, ("req", "seq"), "tensor"),
        P("tensor", ("req", "seq")),
        P(),
        P(None, "tensor"),
        P("tensor"),
        P("tensor"),
        P("tensor"),
        P("req"),
    )
    out_specs = (P("req", "seq", "tensor"), P("req", "seq", "tensor", None))
    return jax.shard_map(local, mesh=mesh, in_specs=in_specs, out_specs=out_specs, check_vma=False)
```

profile of v0, /device:TPU:16, one launch (start us, length us, event | category | flops | bytes accessed | tf_op | source)
XLA Modules:
  0.0 378.8 jit_solution(334898698690711845)
XLA Ops:
  10.7 1.6 convert_bitcast_fusion
  13.4 3.2 collective-permute-start
  17.3 1.7 collective-permute-done.tail_ref
  19.0 1.2 copy-done.8
  22.5 47.7 %mix.1 = (bf16[512,4096]{1,0:T(8,128)(2,1)S(1)}, bf16[512,4096]{1,0:T(8,128)(2,1)}, bf16[512,4096]{1,0:T(8,128)(2,1)}, bf16[512,128]{1,0:T(8,128)(2,1)S(1)}) custom-call(bf16[512,4096]{1,0:T(8,128)(2,1)} %bitcast.44, bf16[2,4096]{1,0:T(2,128)(2,1)S(1)} %collective-permute-done.tail_ref, s32[1,4096]{1,0:T(1,128)S(1)} %bitcast.40, f32[1,4096]{1,0:T(1,128)S(1)} %bitcast.41, ...), custom_call_target="tpu_custom_call" | custom-call | flops 17179869184 | bytes 33554432 | tf_op jit(solution)/shard_map/mix/pallas_call | solution.py:113
  70.3 2.0 copy-done.15
  72.3 20.2 %all-gather.14.cloned.1.call-done = bf16[1,4096,1024]{2,1,0:T(8,128)(2,1)} async-done(((bf16[1,64,1024]{2,1,0:T(8,128)(2,1)}), bf16[1,4096,1024]{2,1,0:T(8,128)(2,1)}) %all-gather.14.cloned.1.call-update) | async-done | bytes 8388624 | tf_op jit(solution)/shard_map/all_gather | solution.py:338
  92.5 10.2 %fusion.12.v_ref = bf16[512,1024]{1,0:T(8,128)(2,1)} fusion(bf16[512,4096]{1,0:T(8,128)(2,1)} %get-tuple-element.13, bf16[1,4096,1024]{2,1,0:T(8,128)(2,1)} %all-gather.14.cloned.1.call-done), kind=kOutput, calls=%fused_computation.10 | convolution fusion | flops 4295491584 | bytes 13631488 | tf_op jit(solution)/shard_map/dot_general | solution.py:36
  102.7 71.6 %all-gather.12.cloned.1.call-done = bf16[1,4096,1024]{2,1,0:T(8,128)(2,1)} async-done(((bf16[1,64,1024]{2,1,0:T(8,128)(2,1)}), bf16[1,4096,1024]{2,1,0:T(8,128)(2,1)}) %all-gather.12.cloned.1.call-update) | async-done | bytes 8388624 | tf_op jit(solution)/shard_map/all_gather | solution.py:337
  174.3 9.2 %fusion.9.k_ref = bf16[512,1024]{1,0:T(8,128)(2,1)S(1)} fusion(bf16[512,4096]{1,0:T(8,128)(2,1)} %get-tuple-element.12, bf16[1,4096,1024]{2,1,0:T(8,128)(2,1)} %all-gather.12.cloned.1.call-done), kind=kOutput, calls=%fused_computation.9 | convolution fusion | flops 4295491584 | bytes 13631488 | tf_op jit(solution)/shard_map/dot_general | solution.py:36
  183.7 9.4 %local_states.1 = (f32[512,1024]{1,0:T(8,128)S(1)}, bf16[2,8,128,128]{3,2,1,0:T(8,128)(2,1)}, f32[2,8,128,128]{3,2,1,0:T(8,128)S(1)}) custom-call(f32[512,128]{1,0:T(8,128)S(1)} %broadcast_in_dim.24.valid_ref, bf16[512,128]{1,0:T(8,128)(2,1)S(1)} %get-tuple-element.14.lora_ref, bf16[128,1024]{1,0:T(8,128)(2,1)S(1)} %copy-done.10, f32[1,1024]{1,0:T(1,128)S(1)} %bitcast.42, ...), custom_call_target="tpu_custom_call" | custom-call | flops 1000000000 | bytes 8388608 | tf_op jit(solution)/shard_map/local_states/pallas_call | solution.py:192
  193.5 3.1 collective-permute-start.2
  196.6 1.3 collective-permute-start.4
  197.9 1.9 collective-permute-start.1
  199.8 1.3 collective-permute-start.3
  201.1 1.5 collective-permute-start.5
  202.6 59.0 %all-gather.10.cloned.1.call-done = bf16[1,4096,1024]{2,1,0:T(8,128)(2,1)} async-done(((bf16[1,64,1024]{2,1,0:T(8,128)(2,1)}), bf16[1,4096,1024]{2,1,0:T(8,128)(2,1)}) %all-gather.10.cloned.1.call-update) | async-done | bytes 8388624 | tf_op jit(solution)/shard_map/all_gather | solution.py:339
  261.6 9.3 %fusion.6.r_ref = bf16[512,1024]{1,0:T(8,128)(2,1)S(1)} fusion(bf16[512,4096]{1,0:T(8,128)(2,1)} %copy-done.15, bf16[1,4096,1024]{2,1,0:T(8,128)(2,1)} %all-gather.10.cloned.1.call-done), kind=kOutput, calls=%fused_computation.8 | convolution fusion | flops 4295491584 | bytes 13631488 | tf_op jit(solution)/shard_map/dot_general | solution.py:36
  271.0 1.8 multiply_add_fusion.in_ref
  272.9 30.1 %read_states.1 = (bf16[512,1024]{1,0:T(8,128)(2,1)S(1)}, f32[2,8,2,64,64]{4,3,2,1,0:T(8,128)S(1)}) custom-call(f32[512,128]{1,0:T(8,128)S(1)} %broadcast_in_dim.24.valid_ref, bf16[512,1024]{1,0:T(8,128)(2,1)S(1)} %fusion.6.r_ref, bf16[512,1024]{1,0:T(8,128)(2,1)S(1)} %copy-done.3, bf16[512,1024]{1,0:T(8,128)(2,1)S(1)} %copy-done.1, ...), custom_call_target="tpu_custom_call" | custom-call | flops 2000000000 | bytes 8388608 | tf_op jit(solution)/shard_map/read_states/pallas_call | solution.py:297
  304.9 37.9 %all-gather.8.cloned.1.call-done = bf16[4096,1024]{1,0:T(8,128)(2,1)} async-done(((bf16[64,1024]{1,0:T(8,128)(2,1)}), bf16[4096,1024]{1,0:T(8,128)(2,1)}) %all-gather.8.cloned.1.call-update) | async-done | bytes 8388624 | tf_op jit(solution)/shard_map/all_gather | solution.py:340
  342.9 10.3 %convolution_convert_fusion = bf16[512,4096]{1,0:T(8,128)(2,1)} fusion(bf16[512,1024]{1,0:T(8,128)(2,1)} %copy-done.9, bf16[4096,1024]{1,0:T(8,128)(2,1)} %all-gather.8.cloned.1.call-done), kind=kOutput, calls=%fused_computation.6 | convolution fusion | flops 4297064448 | bytes 13631488 | tf_op jit(solution)/shard_map/dot_general | solution.py:36
  355.5 12.3 %reduce-scatter.2.cloned.1.call-done = bf16[512,2048]{1,0:T(8,128)(2,1)} async-done(((bf16[512,4096]{1,0:T(8,128)(2,1)}), bf16[512,2048]{1,0:T(8,128)(2,1)}) %reduce-scatter.2.cloned.1.call-update) | async-done | bytes 2097168 | tf_op jit(solution)/shard_map/reduce_scatter | solution.py:369
  367.8 4.4 %add_convert_fusion = bf16[512,2048]{1,0:T(8,128)(2,1)} fusion(bf16[512,2048]{1,0:T(8,128)(2,1)} %reduce-scatter.2.cloned.1.call-done, bf16[512,4096]{1,0:T(8,128)(2,1)} %bitcast.45, s32[]{:T(128)S(6)} %select_n.3), kind=kLoop, calls=%fused_computation.7 | loop fusion | flops 4194304 | bytes 6291460 | tf_op jit(solution)/shard_map/convert_element_type | solution.py:374
  (56 shorter events, 12.4 us)
Async XLA Ops:
  7.2 85.4 %all-gather.14.cloned.1.call-start = ((), (), s32[]{:S(2)}) async-start(), calls=%async_computation.5 | async-start | bytes 8519680 | tf_op jit(solution)/shard_map/all_gather | solution.py:338
  9.2 165.2 %all-gather.12.cloned.1.call-start = ((), (), s32[]{:S(2)}) async-start(), calls=%async_computation.4 | async-start | bytes 8519680 | tf_op jit(solution)/shard_map/all_gather | solution.py:337
  9.9 251.7 %all-gather.10.cloned.1.call-start = ((), (), s32[]{:S(2)}) async-start(), calls=%async_computation.3 | async-start | bytes 8519680 | tf_op jit(solution)/shard_map/all_gather | solution.py:339
  10.7 332.2 %all-gather.8.cloned.1.call-start = ((), (), s32[]{:S(2)}) async-start(), calls=%async_computation.1 | async-start | bytes 8519680 | tf_op jit(solution)/shard_map/all_gather | solution.py:340
  12.4 355.4 %reduce-scatter.2.cloned.1.call-start = ((), (), s32[]{:S(2)}) async-start(), calls=%async_computation.2 | async-start | bytes 6291456 | tf_op jit(solution)/shard_map/reduce_scatter | solution.py:369
  13.4 5.6 %collective-permute-start = (bf16[2,4096]{1,0:T(2,128)(2,1)S(1)}, bf16[2,4096]{1,0:T(2,128)(2,1)S(1)}, u32[]{:S(2)}, u32[]{:S(2)}) collective-permute-start(bf16[2,4096]{1,0:T(2,128)(2,1)S(1)} %bitcast.47), channel_id=1, source_target_pairs={{0,1},{1,2},{2,3},{4,5},{5,6},{6,7},{8,9},{9,10},{10,11},{12,13},{... | collective-permute-start | bytes 49160 | tf_op jit(solution)/shard_map/ppermute | solution.py:26
  19.0 1.2 copy-start.8
  70.3 2.0 copy-start.15
  174.3 9.4 %copy-start = (bf16[512,1024]{1,0:T(8,128)(2,1)S(1)}, bf16[512,1024]{1,0:T(8,128)(2,1)}, u32[]{:S(2)}) copy-start(bf16[512,1024]{1,0:T(8,128)(2,1)} %fusion.12.v_ref) | copy-start | bytes 3145732
  174.3 9.4 %copy-start.10 = (bf16[128,1024]{1,0:T(8,128)(2,1)S(1)}, bf16[128,1024]{1,0:T(8,128)(2,1)}, u32[]{:S(2)}) copy-start(bf16[128,1024]{1,0:T(8,128)(2,1)} %right_ref.1) | copy-start | bytes 786436
  174.3 9.4 %copy-start.14 = (f32[1024]{0:T(1024)S(1)}, f32[1024]{0:T(1024)}, u32[]{:S(2)}) copy-start(f32[1024]{0:T(1024)} %param.20) | copy-start | bytes 12292
  183.6 9.6 %copy-start.2 = (bf16[512,1024]{1,0:T(8,128)(2,1)}, bf16[512,1024]{1,0:T(8,128)(2,1)S(1)}, u32[]{:S(2)}) copy-start(bf16[512,1024]{1,0:T(8,128)(2,1)S(1)} %fusion.9.k_ref) | copy-start | bytes 3145732
  193.5 77.4 %collective-permute-start.2 = (f32[2,8,128]{2,1,0:T(8,128)S(1)}, f32[2,8,128]{2,1,0:T(8,128)S(1)}, u32[]{:S(2)}, u32[]{:S(2)}) collective-permute-start(f32[2,8,128]{2,1,0:T(8,128)S(1)} %slice_reduce_fusion), channel_id=1, source_target_pairs={{0,1},{1,2},{2,3},{4,5},{5,6},{6,7},{8,9},{9,10},{10,11},{12,13},{... | collective-permute-start | bytes 24584 | tf_op jit(solution)/shard_map/ppermute | solution.py:26
  196.6 74.4 %collective-permute-start.4 = (f32[2,8,128]{2,1,0:T(8,128)S(1)}, f32[2,8,128]{2,1,0:T(8,128)S(1)}, u32[]{:S(2)}, u32[]{:S(2)}) collective-permute-start(f32[2,8,128]{2,1,0:T(8,128)S(1)} %slice_reduce_fusion), channel_id=1, source_target_pairs={{0,2},{1,3},{4,6},{5,7},{8,10},{9,11},{12,14},{13,15},{16,18},{17,... | collective-permute-start | bytes 24584 | tf_op jit(solution)/shard_map/ppermute | solution.py:26
  197.9 73.1 %collective-permute-start.1 = (bf16[2,8,128,128]{3,2,1,0:T(8,128)(2,1)}, bf16[2,8,128,128]{3,2,1,0:T(8,128)(2,1)}, u32[]{:S(2)}, u32[]{:S(2)}) collective-permute-start(bf16[2,8,128,128]{3,2,1,0:T(8,128)(2,1)} %get-tuple-element.16.l_ref), channel_id=1, source_target_pairs={{0,1},{1,2},{2,3},{4,5},{5,6},{6,7},{8,9},{9,10},{10,11},{12,13},{... | collective-permute-start | bytes 1572872 | tf_op jit(solution)/shard_map/ppermute | solution.py:26
  199.8 71.2 %collective-permute-start.3 = (bf16[2,8,128,128]{3,2,1,0:T(8,128)(2,1)}, bf16[2,8,128,128]{3,2,1,0:T(8,128)(2,1)}, u32[]{:S(2)}, u32[]{:S(2)}) collective-permute-start(bf16[2,8,128,128]{3,2,1,0:T(8,128)(2,1)} %get-tuple-element.16.l_ref), channel_id=1, source_target_pairs={{0,2},{1,3},{4,6},{5,7},{8,10},{9,11},{12,14},{13,15},{16,18},{17,... | collective-permute-start | bytes 1572872 | tf_op jit(solution)/shard_map/ppermute | solution.py:26
  201.1 69.9 %collective-permute-start.5 = (bf16[2,8,128,128]{3,2,1,0:T(8,128)(2,1)}, bf16[2,8,128,128]{3,2,1,0:T(8,128)(2,1)}, u32[]{:S(2)}, u32[]{:S(2)}) collective-permute-start(bf16[2,8,128,128]{3,2,1,0:T(8,128)(2,1)} %get-tuple-element.16.l_ref), channel_id=1, source_target_pairs={{0,3},{4,7},{8,11},{12,15},{16,19},{20,23},{24,27},{28,31},{32,35}... | collective-permute-start | bytes 1572872 | tf_op jit(solution)/shard_map/ppermute | solution.py:26
  261.6 11.2 %copy-start.1 = (bf16[512,1024]{1,0:T(8,128)(2,1)S(1)}, bf16[512,1024]{1,0:T(8,128)(2,1)}, u32[]{:S(2)}) copy-start(bf16[512,1024]{1,0:T(8,128)(2,1)} %fusion.12.v_ref) | copy-start | bytes 3145732
  261.6 11.2 %copy-start.3 = (bf16[512,1024]{1,0:T(8,128)(2,1)S(1)}, bf16[512,1024]{1,0:T(8,128)(2,1)}, u32[]{:S(2)}) copy-start(bf16[512,1024]{1,0:T(8,128)(2,1)} %copy-done.2) | copy-start | bytes 3145732
  261.6 11.2 %copy-start.6 = (f32[1024]{0:T(1024)S(1)}, f32[1024]{0:T(1024)}, u32[]{:S(2)}) copy-start(f32[1024]{0:T(1024)} %param.21) | copy-start | bytes 12292
  261.6 11.2 %copy-start.7 = (f32[1024]{0:T(1024)S(1)}, f32[1024]{0:T(1024)}, u32[]{:S(2)}) copy-start(f32[1024]{0:T(1024)} %param.22) | copy-start | bytes 12292
  303.0 1.0 copy-start.4
  304.0 1.0 copy-start.9
  353.1 1.2 copy-start.5
  (3 other events, 2.3 us)
Sparse Core Ops, SparseCore 0:
  11.5 81.0 all-gather.13
  96.0 78.2 all-gather.11
  177.2 84.3 all-gather.9
  264.4 78.4 all-gather.7
  353.3 14.4 reduce-scatter.1
where the time goes:
time: 381 us; the launch traced here: 379 us
  waiting for transfers between devices  204 us (54%)
  Pallas kernels  87.2 us (23%)
  matrix products  38.9 us (10%)
  between operations  14 us (4%)
  starting transfers between devices  12.5 us (3%)
  local copies, waits for them, and re-layouts  12.1 us (3%)
  other arithmetic  9.81 us (3%)
    all_gather x1, waiting for transfers between devices, local(): weight_k = gather(weights[1], axis=0)  71.6 us
    all_gather x1, waiting for transfers between devices, local(): weight_r = gather(weights[0], axis=0)  59 us
    pallas_call x1, Pallas kernels, mix(): pl.pallas_call(mix_kernel, grid=(width // COLS,), in_specs=[whole((rows,...  47.7 us
    dot_general x4, matrix products, dot32(): return lax.dot_general(a, b, dims, preferred_element_type=f32)  38.9 us
    all_gather x1, waiting for transfers between devices, local(): weight_out = gather(learner_projection_slices.T.astype(bf16), axis=0)  37.9 us
    pallas_call x1, Pallas kernels, read_states(): pl.pallas_call(functools.partial(read_kernel, span), grid=(pairs,), in_sp...  30.1 us
    all_gather x1, waiting for transfers between devices, local(): weight_v = gather(weights[2], axis=0)  20.2 us
    reduce_scatter x1, waiting for transfers between devices, local(): lax.psum_scatter(terms.astype(bf16), 'tensor', scatter_dimension=1, tiled...  12.3 us
  transfers between devices with their start and end apart: 11, of which 6 were waited for; matrix products, arithmetic and copies ran while one was open for 9% of the time, Pallas kernels for 23%

commit v1 on v0

--- a/solution.py
+++ b/solution.py
@@ -10,7 +10,6 @@
 ATTEND_DIM = 64
 PAIR = 128
 CHUNK = 128
-COLS = 256
 SAFE = -60.0
 eps = 1e-05
 f32 = jnp.float32
@@ -36,105 +35,276 @@
     return lax.dot_general(a, b, dims, preferred_element_type=f32)
 
 
-def mix_kernel(
-    x_ref, tail_ref, perm_ref, gain_ref, blend_ref, left_ref, mr_ref, mk_ref, mv_ref, lora_ref,
-    stack, chosen, stats, low_rank,
+MESH = pl.DeviceIdType.MESH
+ORDERS = (("x", "y", "z"), ("y", "z", "x"), ("z", "x", "y"))
+PLACES = (("z", "y", "x"), ("x", "y", "z"), ("y", "x", "z"))
+SIDE = 4
+STEP = 512
+
+
+def position():
+    req = lax.axis_index("req")
+    return {"x": req // SIDE, "z": req % SIDE, "y": lax.axis_index("seq")}
+
+
+def moved(at, axis, by):
+    return {**at, axis: (at[axis] + by + SIDE) % SIDE}
+
+
+def device(at):
+    return (lax.axis_index("tensor"), at["x"] * SIDE + at["z"], at["y"])
+
+
+def greet_neighbours(at):
+    barrier = pltpu.get_barrier_semaphore()
+    for axis in "xyz":
+        for by in (1, -1):
+            pl.semaphore_signal(
+                barrier, inc=1, device_id=device(moved(at, axis, by)), device_id_type=MESH
+            )
+    pl.semaphore_wait(barrier, 6)
+
+
+class Ring:
+    def __init__(self, slots, order, places, send, recv, parts):
+        self.slots, self.order, self.places = slots, order, places
+        self.send, self.recv, self.parts = send, recv, parts
+        self.at = position()
+
+    def block(self, phase, where, part):
+        index = []
+        for axis in self.places:
+            turn = self.order.index(axis)
+            index.append(slice(None) if turn < phase else where if turn == phase else self.at[axis])
+        return self.slots.at[(*index, *part)]
+
+    def copy(self, phase, kind, right):
+        axis = self.order[phase]
+        to = moved(self.at, axis, 1 if right else -1)
+        if kind == 0:
+            ref = self.block(phase, self.at[axis], ())
+        else:
+            source = moved(self.at, axis, -1 if right else 1)[axis]
+            ref = self.block(phase, source, (self.parts[0 if right else 1],))
+        slot = 2 * kind + (0 if right else 1)
+        return pltpu.make_async_remote_copy(
+            ref, ref, self.send.at[phase, slot], self.recv.at[phase, slot],
+            device_id=device(to), device_id_type=MESH,
+        )
+
+    def start(self, phase, kind):
+        for right in (True, False):
+            self.copy(phase, kind, right).start()
+
+    def arrived(self, phase, kind):
+        for right in (True, False):
+            self.copy(phase, kind, right).wait_recv()
+
+    def finish(self):
+        for phase in range(3):
+            for kind in range(2):
+                for right in (True, False):
+                    self.copy(phase, kind, right).wait_send()
+
+
+def project_kernel(
+    x_ref, last_ref, perm_ref, gain_ref, blend_ref, left_ref, w_ref, out_ref, lora_ref,
+    slots, stack, mixed, chosen, picked, total, stats, low_rank, tail, load_sem, tail_sem, send, recv,
 ):
     rows, width = x_ref.shape
-    span = rows // tail_ref.shape[0]
-    step = pl.program_id(0)
-
-    @pl.when(step == 0)
-    def _():
-        stack[:rows, :] = x_ref[...]
-        table = jnp.concatenate([gain_ref[...], blend_ref[0:3, :]], axis=0)
-        first = table.astype(bf16)
-        rest = table - first.astype(f32)
-        second = rest.astype(bf16)
-        third = (rest - second.astype(f32)).astype(bf16)
-        pad = jnp.zeros((2, width), bf16)
-        stack[rows:, :] = jnp.concatenate([tail_ref[...], first, second, third, pad], axis=0)
-        low_rank[...] = jnp.zeros_like(low_rank)
-
-        def row_stats(i, _):
-            at = pl.ds(pl.multiple_of(i * 16, 16), 16)
-            part = stack[at, :].astype(f32)
-            mean = jnp.mean(part, axis=-1, keepdims=True)
-            centred = part - mean
-            spread = jnp.mean(centred * centred, axis=-1, keepdims=True)
-            stats[0, at, :] = jnp.broadcast_to(mean, (16, PAIR))
-            stats[1, at, :] = jnp.broadcast_to(lax.rsqrt(spread + eps), (16, PAIR))
-            return 0
-
-        lax.fori_loop(0, stack.shape[0] // 16, row_stats, 0)
-
-    mean, scale = stats[0, :, 0:1], stats[1, :, 0:1]
-    row = lax.broadcasted_iota(jnp.int32, (rows, 1), 0)
+    reqs = last_ref.shape[0]
+    span = rows // reqs
+    at = position()
+    half = w_ref.shape[1] // 2
+    parts = (slice(0, half), slice(half, 2 * half))
+    rings = [
+        Ring(slots.at[m], ORDERS[m], PLACES[m], send.at[m], recv.at[m], parts) for m in range(3)
+    ]
+    load = pltpu.make_async_copy(x_ref, stack.at[pl.ds(0, rows)], load_sem)
+    load.start()
+    for m in range(3):
+        slots[(m, *(at[axis] for axis in PLACES[m]))] = w_ref[m].astype(bf16)
+    greet_neighbours(at)
+    hand_on = pltpu.make_async_remote_copy(
+        last_ref, tail, tail_sem.at[0], tail_sem.at[1],
+        device_id=device(moved(at, "y", 1)), device_id_type=MESH,
+    )
+    hand_on.start()
+    for ring in rings:
+        ring.start(0, 0)
+
+    table = jnp.concatenate([gain_ref[...], blend_ref[0:3, :]], axis=0)
+    first = table.astype(bf16)
+    rest = table - first.astype(f32)
+    second = rest.astype(bf16)
+    third = (rest - second.astype(f32)).astype(bf16)
+    hand_on.wait_recv()
+    before = jnp.where(at["y"] > 0, tail[...].astype(f32), 0.0).astype(bf16)
+    pad = jnp.zeros((16 - reqs - 12, width), bf16)
+    stack[rows:, :] = jnp.concatenate([before, first, second, third, pad], axis=0)
+    low_rank[...] = jnp.zeros_like(low_rank)
+    load.wait()
+
+    def row_stats(i, _):
+        here = pl.ds(pl.multiple_of(i * 16, 16), 16)
+        part = stack[here, :].astype(f32)
+        mean = jnp.mean(part, axis=-1, keepdims=True)
+        centred = part - mean
+        spread = jnp.mean(centred * centred, axis=-1, keepdims=True)
+        stats[0, here, :] = jnp.broadcast_to(mean, (16, PAIR))
+        stats[1, here, :] = jnp.broadcast_to(lax.rsqrt(spread + eps), (16, PAIR))
+        return 0
+
+    lax.fori_loop(0, stack.shape[0] // 16, row_stats, 0)
 
     def shifted(values, gain):
-        normal = (values - mean[: values.shape[0]]) * scale[: values.shape[0]] * gain
+        mean, scale = stats[0, :, 0:1], stats[1, :, 0:1]
+        row = lax.broadcasted_iota(jnp.int32, (rows, 1), 0)
+        normal = (values - mean) * scale * gain
         current = normal[:rows]
         previous = pltpu.roll(current, 1, axis=0)
-        for b in range(rows // span):
+        for b in range(reqs):
             previous = jnp.where(row == b * span, normal[rows + b : rows + b + 1], previous)
         return current, previous - current
 
-    names = perm_ref[...]
-
-    def one_hot(i, _):
-        base = pl.multiple_of(i * COLS, COLS)
-        feature = lax.broadcasted_iota(jnp.int32, (COLS, COLS), 0) + base
-        chosen[pl.ds(base, COLS), :] = (feature == names).astype(f32).astype(bf16)
+    piece = STEP // 2
+    depth = chosen.shape[0]
+
+    def mix_step(step, _):
+        here = pl.ds(pl.multiple_of(step * STEP, STEP), STEP)
+        names = perm_ref[:, here]
+        picked[...] = jnp.zeros_like(picked)
+
+        def pick(d, _):
+            def one_hot(i, _):
+                base = pl.multiple_of(i * 128, 128)
+                feature = lax.broadcasted_iota(jnp.int32, (128, STEP), 0) + (base + d * depth)
+                chosen[pl.ds(base, 128), :] = (feature == names).astype(f32).astype(bf16)
+                return 0
+
+            lax.fori_loop(0, depth // 128, one_hot, 0)
+            source = stack[:, pl.ds(pl.multiple_of(d * depth, depth), depth)]
+            picked[...] += dot32(source, chosen[...])
+            return 0
+
+        lax.fori_loop(0, width // depth, pick, 0)
+        y, x0 = step // 2, (step % 2) * 2
+        for i in range(2):
+            values = picked[:, i * piece : (i + 1) * piece]
+            own = values[rows + reqs :]
+            own = own[0:4] + own[4:8] + own[8:12]
+            current, delta = shifted(values, own[0:1])
+            blended = [(current + delta * own[1 + j : 2 + j]).astype(bf16) for j in range(3)]
+            picked[:rows, i * piece : (i + 1) * piece] = blended[0].astype(f32)
+            mixed[1, x0 + i, :, pl.ds(pl.multiple_of(y * piece, piece), piece)] = blended[1]
+            mixed[2, y, :, pl.ds(pl.multiple_of((x0 + i) * piece, piece), piece)] = blended[2]
+        columns = pl.ds(pl.multiple_of(step * 128, 128), 128)
+        for z in range(SIDE):
+            pair = [picked[:rows, i * piece + z * 64 : i * piece + (z + 1) * 64] for i in range(2)]
+            mixed[0, z, :, columns] = jnp.concatenate(pair, axis=1).astype(bf16)
+
+        current, delta = shifted(stack[:, here].astype(f32), gain_ref[:, here])
+        low_rank[...] += dot32(
+            (current + delta * blend_ref[3:4, here]).astype(bf16),
+            left_ref[pl.ds(pl.multiple_of(step * STEP, STEP), STEP), :],
+        )
+
+        @pl.when(step == 0)
+        def _():
+            for ring in rings:
+                ring.arrived(0, 0)
+                ring.start(0, 1)
+
+        @pl.when(step == 1)
+        def _():
+            for ring in rings:
+                ring.arrived(0, 1)
+                ring.start(1, 0)
+
+        @pl.when(step == 3)
+        def _():
+            for ring in rings:
+                ring.arrived(1, 0)
+                ring.start(1, 1)
+
+        @pl.when(step == 4)
+        def _():
+            for ring in rings:
+                ring.arrived(1, 1)
+                ring.start(2, 0)
+
         return 0
 
-    lax.fori_loop(0, width // COLS, one_hot, 0)
-    picked = dot32(stack[...], chosen[...])
-    table = picked[rows + 2 : rows + 6] + picked[rows + 6 : rows + 10] + picked[rows + 10 : rows + 14]
-    current, delta = shifted(picked, table[0:1])
-    mr_ref[...] = (current + delta * table[1:2]).astype(bf16)
-    mk_ref[...] = (current + delta * table[2:3]).astype(bf16)
-    mv_ref[...] = (current + delta * table[3:4]).astype(bf16)
-
-    here = pl.ds(pl.multiple_of(step * COLS, COLS), COLS)
-    current, delta = shifted(stack[:, here].astype(f32), gain_ref[:, here])
-    mixed = (current + delta * blend_ref[3:4, here]).astype(bf16)
-    low_rank[...] += dot32(mixed, left_ref[...])
-
-    @pl.when(step == pl.num_programs(0) - 1)
-    def _():
-        lora_ref[...] = jnp.tanh(low_rank[...]).astype(bf16)
-
-
-def mix(x, tail, perm, gain, blend, left):
+    lax.fori_loop(0, width // STEP, mix_step, 0)
+    lora_ref[...] = jnp.tanh(low_rank[...]).astype(bf16)
+
+    def products(offset, fresh):
+        def tile(i, _):
+            m, n = i // 4, i % 4
+            own = jnp.where(m == 0, at["z"], jnp.where(m == 1, at["x"], at["y"]))
+            plane = (own + offset) % SIDE
+            here = pl.ds(pl.multiple_of(n * 256, 256), 256)
+            weight = slots[m, plane, :, :, :, here].reshape(width // SIDE, 256)
+            product = dot32(mixed[m, plane], weight)
+            if fresh:
+                total[m, :, here] = product
+            elif offset == 2:
+                out_ref[m, :, here] = (total[m, :, here] + product).astype(bf16)
+            else:
+                total[m, :, here] += product
+            return 0
+
+        lax.fori_loop(0, 12, tile, 0)
+
+    products(0, True)
+    for ring in rings:
+        ring.arrived(2, 0)
+        ring.start(2, 1)
+    products(1, False)
+    products(3, False)
+    for ring in rings:
+        ring.arrived(2, 1)
+    products(2, False)
+    hand_on.wait_send()
+    for ring in rings:
+        ring.finish()
+
+
+def project(x, last, perm, gain, blend, left, weights):
     rows, width = x.shape
-    whole = lambda shape: pl.BlockSpec(shape, lambda i: (0,) * len(shape))
-    column = pl.BlockSpec((rows, COLS), lambda i: (0, i))
-    out = jax.ShapeDtypeStruct((rows, width), bf16)
+    inner, local_width = left.shape[1], weights.shape[2]
+    vmem = pl.BlockSpec(memory_space=pltpu.VMEM)
     return pl.pallas_call(
-        mix_kernel,
-        grid=(width // COLS,),
-        in_specs=[
-            whole((rows, width)),
-            whole(tail.shape),
-            pl.BlockSpec((1, COLS), lambda i: (0, i)),
-            whole((1, width)),
-            whole((4, width)),
-            pl.BlockSpec((COLS, left.shape[1]), lambda i: (i, 0)),
+        project_kernel,
+        in_specs=[pl.BlockSpec(memory_space=pl.ANY)] + [vmem] * 6,
+        out_specs=[vmem, vmem],
+        out_shape=[
+            jax.ShapeDtypeStruct((3, rows, local_width), bf16),
+            jax.ShapeDtypeStruct((rows, inner), bf16),
         ],
-        out_specs=[column, column, column, whole((rows, left.shape[1]))],
-        out_shape=[out, out, out, jax.ShapeDtypeStruct((rows, left.shape[1]), bf16)],
         scratch_shapes=[
+            pltpu.VMEM((3, SIDE, SIDE, SIDE, *weights.shape[1:]), bf16),
             pltpu.VMEM((rows + 16, width), bf16),
-            pltpu.VMEM((width, COLS), bf16),
+            pltpu.VMEM((3, SIDE, rows, width // SIDE), bf16),
+            pltpu.VMEM((width // 2, STEP), bf16),
+            pltpu.VMEM((rows + 16, STEP), f32),
+            pltpu.VMEM((3, rows, local_width), f32),
             pltpu.VMEM((2, rows + 16, PAIR), f32),
-            pltpu.VMEM((rows, left.shape[1]), f32),
+            pltpu.VMEM((rows, inner), f32),
+            pltpu.VMEM(last.shape, bf16),
+            pltpu.SemaphoreType.DMA,
+            pltpu.SemaphoreType.DMA((2,)),
+            pltpu.SemaphoreType.DMA((3, 3, 4)),
+            pltpu.SemaphoreType.DMA((3, 3, 4)),
         ],
-        compiler_params=pltpu.CompilerParams(vmem_limit_bytes=48 << 20),
+        compiler_params=pltpu.CompilerParams(
+            collective_id=0, has_side_effects=True, vmem_limit_bytes=61 << 20
+        ),
         cost_estimate=pl.CostEstimate(
-            flops=2 * rows * width * width, bytes_accessed=16 * rows * width, transcendentals=0
+            flops=100 * 10**9, bytes_accessed=32 << 20, transcendentals=0
         ),
-        name="mix",
-    )(x, tail, perm, gain, blend, left)
+        name="project",
+    )(x, last, perm, gain, blend, left, weights)
 
 
 def earlier(size):
@@ -330,24 +500,21 @@
     reqs, span, width = incoming_activations.shape
     rows = reqs * span
     local_width = feature_fading_speed.shape[0]
-    pairs = local_width // PAIR
     x = incoming_activations.reshape(rows, width)
-    weights = learner_acceptor_lookup_slices.astype(bf16)
-    gather = functools.partial(lax.all_gather, axis_name=("req", "seq"), tiled=True)
-    weight_k = gather(weights[1], axis=0)
-    weight_v = gather(weights[2], axis=0)
-    weight_r = gather(weights[0], axis=0)
-    weight_out = gather(learner_projection_slices.T.astype(bf16), axis=0)
-    tail = from_behind(incoming_activations[:, span - 1, :], "seq", 1)
+    weight_out = lax.all_gather(
+        learner_projection_slices.T.astype(bf16), ("req", "seq"), axis=0, tiled=True
+    )
     positions = lax.axis_index("seq") * span + jnp.arange(span, dtype=jnp.int32)
     valid = (positions[None, :] < prompt_extents[:, None]).astype(f32).reshape(rows, 1)
     valid = jnp.broadcast_to(valid, (rows, PAIR))
-    mixed_r, mixed_k, mixed_v, lora = mix(
-        x, tail, learner_line_permutation[None], standardize_scaling[None],
-        lagged_blending_weights, fading_left_matrix,
+    shard = learner_acceptor_lookup_slices.shape[1]
+    perm = learner_line_permutation.reshape(SIDE * SIDE, SIDE, shard).transpose(1, 0, 2)
+    projected, lora = project(
+        x, incoming_activations[:, span - 1, :], perm.reshape(1, width),
+        standardize_scaling[None], lagged_blending_weights, fading_left_matrix,
+        learner_acceptor_lookup_slices,
     )
-    k = dot32(mixed_k, weight_k).astype(bf16)
-    v = dot32(mixed_v, weight_v).astype(bf16)
+    r, k, v = projected
     decays, states, totals = local_states(
         valid, lora, fading_right_matrix, feature_fading_speed[None], k, v, span
     )
@@ -359,7 +526,6 @@
         if by + 1 < lax.axis_size("seq"):
             far_total = from_behind(totals[..., 0], "seq", by)
             sent = sent + far_total[..., None]
-    r = dot32(mixed_r, weight_r).astype(bf16)
     normed, final = read_states(
         valid, r, k, v, decays, incoming, states, totals,
         self_reward[None], cluster_scaling_vector[None], span,

time: 381 us -> 271 us (0.71)
  waiting for transfers between devices: 204 us -> 31.7 us
  Pallas kernels: 87.2 us -> 191 us
  matrix products: 38.9 us -> 9.48 us
  local copies, waits for them, and re-layouts: 12.1 us -> 6.92 us
    all_gather x4 -> x1, waiting for transfers between devices: 189 us -> 0.02 us  [local(): lax.all_gather(learner_projection_slices.T.astype(bf16), ('req', 'seq'),...]
    pallas_call x1, Pallas kernels: 47.7 us -> 152 us  [project(): pl.pallas_call(project_kernel, in_specs=[pl.BlockSpec(memory_space=pl.ANY...]
    dot_general x4 -> x1, matrix products: 38.9 us -> 9.48 us  [dot32(): return lax.dot_general(a, b, dims, preferred_element_type=f32)]
    ppermute x6 -> x5, waiting for transfers between devices: 1.7 us -> 16.9 us  [from_behind(): return lax.ppermute(value, axis, pairs)]
    unnamed x34 -> x12, local copies, waits for them, and re-layouts: 8.76 us -> 0.67 us
    ppermute x6 -> x5, starting transfers between devices: 12.3 us -> 8.69 us  [from_behind(): return lax.ppermute(value, axis, pairs)]
  transfers between devices with their start and end apart: 11 -> 7, of which waited for: 6 -> 3; matrix products, arithmetic and copies ran while one was open for 9% -> 3% of each run, Pallas kernels for 23% -> 71%
where the time goes in v1:
time: 271 us; the launch traced here: 269 us
  Pallas kernels  191 us (70%)
  waiting for transfers between devices  31.7 us (12%)
  between operations  14.3 us (5%)
  matrix products  9.48 us (3%)
  starting transfers between devices  8.77 us (3%)
  other arithmetic  7.51 us (3%)
  local copies, waits for them, and re-layouts  6.92 us (3%)
    pallas_call x1, Pallas kernels, project(): pl.pallas_call(project_kernel, in_specs=[pl.BlockSpec(memory_space=pl.ANY...  152 us
    pallas_call x1, Pallas kernels, read_states(): pl.pallas_call(functools.partial(read_kernel, span), grid=(pairs,), in_sp...  29.4 us
    ppermute x5, waiting for transfers between devices, from_behind(): return lax.ppermute(value, axis, pairs)  16.9 us
    reduce_scatter x1, waiting for transfers between devices, local(): lax.psum_scatter(terms.astype(bf16), 'tensor', scatter_dimension=1, tiled...  14.7 us
    dot_general x1, matrix products, dot32(): return lax.dot_general(a, b, dims, preferred_element_type=f32)  9.48 us
    pallas_call x1, Pallas kernels, local_states(): pl.pallas_call(functools.partial(state_kernel, span), grid=(pairs,), in_s...  8.81 us
    ppermute x5, starting transfers between devices, from_behind(): return lax.ppermute(value, axis, pairs)  8.69 us
  transfers between devices with their start and end apart: 7, of which 3 were waited for; matrix products, arithmetic and copies ran while one was open for 3% of the time, Pallas kernels for 71%

profile of v1, /device:TPU:16, one launch (start us, length us, event | category | flops | bytes accessed | tf_op | source)
XLA Modules:
  0.0 269.3 jit_solution(15084535082765129039)
XLA Ops:
  7.2 1.6 convert_bitcast_fusion
  8.9 0.8 reshape.45
  9.7 0.7 reshape.46.perm_ref
  10.4 0.9 slice.7
  11.3 0.6 copy.22
  12.0 0.7 fusion
  12.7 152.4 %project.1 = (bf16[3,512,1024]{2,1,0:T(8,128)(2,1)}, bf16[512,128]{1,0:T(8,128)(2,1)}) custom-call(bf16[512,4096]{1,0:T(8,128)(2,1)} %bitcast.30, bf16[2,4096]{1,0:T(2,128)(2,1)} %bitcast.34, s32[1,4096]{1,0:T(1,128)} %reshape.46.perm_ref, f32[1,4096]{1,0:T(1,128)} %bitcast.36, f32[4,4096]{1,0:T(4,128)} %blend_ref.1, bf16[4096,128]{1,0:T(8,128)(2,1)} %left_ref.1, ...), custom_call_target="tpu_custom_call" | custom-call | flops 99999997952 | bytes 33554432 | tf_op jit(solution)/shard_map/project/pallas_call | solution.py:277
  165.2 2.2 slice_bitcast_fusion
  167.4 0.1 broadcast_in_dim.10.valid_ref
  167.6 8.8 %local_states.1 = (f32[512,1024]{1,0:T(8,128)S(1)}, bf16[2,8,128,128]{3,2,1,0:T(8,128)(2,1)S(1)}, f32[2,8,128,128]{3,2,1,0:T(8,128)S(1)}) custom-call(f32[512,128]{1,0:T(8,128)S(1)} %broadcast_in_dim.10.valid_ref, bf16[512,128]{1,0:T(8,128)(2,1)S(1)} %copy-done.4, bf16[128,1024]{1,0:T(8,128)(2,1)S(1)} %copy-done.2, f32[1,1024]{1,0:T(1,128)S(1)} %bitcast.28, ...), custom_call_target="tpu_custom_call" | custom-call | flops 1000000000 | bytes 8388608 | tf_op jit(solution)/shard_map/local_states/pallas_call | solution.py:362
  176.4 3.3 %collective-permute-start = (bf16[2,8,128,128]{3,2,1,0:T(8,128)(2,1)S(1)}, bf16[2,8,128,128]{3,2,1,0:T(8,128)(2,1)S(1)}, u32[]{:S(2)}, u32[]{:S(2)}) collective-permute-start(bf16[2,8,128,128]{3,2,1,0:T(8,128)(2,1)S(1)} %get-tuple-element.12.l_ref), channel_id=1, source_target_pairs={{0,1},{1,2},{2,3},{4,5},{5,6},{6,7},{8,9},{9,10},{10,11},{12,13},{... | collective-permute-start | bytes 1572872 | tf_op jit(solution)/shard_map/ppermute | solution.py:25
  179.7 1.3 collective-permute-start.2
  181.0 0.7 collective-permute-start.4
  181.7 0.3 slice_reduce_fusion
  182.0 1.9 collective-permute-start.1
  184.0 1.5 collective-permute-start.3
  185.4 5.9 %collective-permute-done.1 = f32[2,8,128]{2,1,0:T(8,128)S(1)} collective-permute-done((f32[2,8,128]{2,1,0:T(8,128)S(1)}, f32[2,8,128]{2,1,0:T(8,128)S(1)}, u32[]{:S(2)}, u32[]{:S(2)}) %collective-permute-start.1) | collective-permute-done | bytes 8224 | tf_op jit(solution)/shard_map/ppermute | solution.py:25
  191.4 11.0 %collective-permute-done.3 = f32[2,8,128]{2,1,0:T(8,128)S(1)} collective-permute-done((f32[2,8,128]{2,1,0:T(8,128)S(1)}, f32[2,8,128]{2,1,0:T(8,128)S(1)}, u32[]{:S(2)}, u32[]{:S(2)}) %collective-permute-start.3) | collective-permute-done | bytes 8224 | tf_op jit(solution)/shard_map/ppermute | solution.py:25
  202.4 0.7 multiply_add_fusion.in_ref
  203.1 29.4 %read_states.1 = (bf16[512,1024]{1,0:T(8,128)(2,1)S(1)}, f32[2,8,2,64,64]{4,3,2,1,0:T(8,128)S(1)}) custom-call(f32[512,128]{1,0:T(8,128)S(1)} %broadcast_in_dim.10.valid_ref, bf16[512,1024]{1,0:T(8,128)(2,1)S(1)} %get-tuple-element.22.r_ref, bf16[512,1024]{1,0:T(8,128)(2,1)S(1)} %get-tuple-element.21.k_ref, bf16[512,1024]{1,0:T(8,128)(2,1)S(1)} %get-tuple-element.20.v_ref, ...), custom_call_target="tpu_custom_call" | custom-call | flops 2000000000 | bytes 8388608 | tf_op jit(solution)/shard_map/read_states/pallas_call | solution.py:467
  232.6 9.5 %convolution_convert_fusion = bf16[512,4096]{1,0:T(8,128)(2,1)} fusion(bf16[512,1024]{1,0:T(8,128)(2,1)S(1)} %get-tuple-element.14, bf16[4096,1024]{1,0:T(8,128)(2,1)} %all-gather.2.cloned.1.call-done), kind=kOutput, calls=%fused_computation | convolution fusion | flops 4297064448 | bytes 13631488 | tf_op jit(solution)/shard_map/dot_general | solution.py:35
  242.1 1.2 reshape.48
  243.2 14.7 %reduce-scatter.2.cloned.1.call-done = bf16[512,2048]{1,0:T(8,128)(2,1)} async-done(((bf16[512,4096]{1,0:T(8,128)(2,1)}), bf16[512,2048]{1,0:T(8,128)(2,1)}) %reduce-scatter.2.cloned.1.call-update) | async-done | bytes 2097168 | tf_op jit(solution)/shard_map/reduce_scatter | solution.py:535
  258.0 4.4 %add_convert_fusion = bf16[512,2048]{1,0:T(8,128)(2,1)} fusion(bf16[512,2048]{1,0:T(8,128)(2,1)} %reduce-scatter.2.cloned.1.call-done, bf16[512,4096]{1,0:T(8,128)(2,1)} %bitcast.31, s32[]{:T(128)S(6)} %select_n.3), kind=kLoop, calls=%fused_computation.1 | loop fusion | flops 4194304 | bytes 6291460 | tf_op jit(solution)/shard_map/convert_element_type | solution.py:540
  (22 shorter events, 0.2 us)
Async XLA Ops:
  7.2 225.4 %all-gather.2.cloned.1.call-start = ((), (), s32[]{:S(2)}) async-start(), calls=%async_computation.1 | async-start | bytes 8519680 | tf_op jit(solution)/shard_map/all_gather | solution.py:504
  8.9 249.1 %reduce-scatter.2.cloned.1.call-start = ((), (), s32[]{:S(2)}) async-start(), calls=%async_computation.2 | async-start | bytes 6291456 | tf_op jit(solution)/shard_map/reduce_scatter | solution.py:535
  165.1 2.4 copy-start.2
  165.1 2.4 copy-start.3
  165.2 2.4 copy-start.4
  167.4 35.7 %copy-start = (f32[1024]{0:T(1024)S(1)}, f32[1024]{0:T(1024)}, u32[]{:S(2)}) copy-start(f32[1024]{0:T(1024)} %param.21) | copy-start | bytes 12292
  167.4 35.7 %copy-start.1 = (f32[1024]{0:T(1024)S(1)}, f32[1024]{0:T(1024)}, u32[]{:S(2)}) copy-start(f32[1024]{0:T(1024)} %param.22) | copy-start | bytes 12292
  176.4 26.0 %collective-permute-start = (bf16[2,8,128,128]{3,2,1,0:T(8,128)(2,1)S(1)}, bf16[2,8,128,128]{3,2,1,0:T(8,128)(2,1)S(1)}, u32[]{:S(2)}, u32[]{:S(2)}) collective-permute-start(bf16[2,8,128,128]{3,2,1,0:T(8,128)(2,1)S(1)} %get-tuple-element.12.l_ref), channel_id=1, source_target_pairs={{0,1},{1,2},{2,3},{4,5},{5,6},{6,7},{8,9},{9,10},{10,11},{12,13},{... | collective-permute-start | bytes 1572872 | tf_op jit(solution)/shard_map/ppermute | solution.py:25
  179.7 22.7 %collective-permute-start.2 = (bf16[2,8,128,128]{3,2,1,0:T(8,128)(2,1)S(1)}, bf16[2,8,128,128]{3,2,1,0:T(8,128)(2,1)S(1)}, u32[]{:S(2)}, u32[]{:S(2)}) collective-permute-start(bf16[2,8,128,128]{3,2,1,0:T(8,128)(2,1)S(1)} %get-tuple-element.12.l_ref), channel_id=1, source_target_pairs={{0,2},{1,3},{4,6},{5,7},{8,10},{9,11},{12,14},{13,15},{16,18},{17,... | collective-permute-start | bytes 1572872 | tf_op jit(solution)/shard_map/ppermute | solution.py:25
  181.0 21.4 %collective-permute-start.4 = (bf16[2,8,128,128]{3,2,1,0:T(8,128)(2,1)S(1)}, bf16[2,8,128,128]{3,2,1,0:T(8,128)(2,1)S(1)}, u32[]{:S(2)}, u32[]{:S(2)}) collective-permute-start(bf16[2,8,128,128]{3,2,1,0:T(8,128)(2,1)S(1)} %get-tuple-element.12.l_ref), channel_id=1, source_target_pairs={{0,3},{4,7},{8,11},{12,15},{16,19},{20,23},{24,27},{28,31},{32,35}... | collective-permute-start | bytes 1572872 | tf_op jit(solution)/shard_map/ppermute | solution.py:25
  182.0 9.3 %collective-permute-start.1 = (f32[2,8,128]{2,1,0:T(8,128)S(1)}, f32[2,8,128]{2,1,0:T(8,128)S(1)}, u32[]{:S(2)}, u32[]{:S(2)}) collective-permute-start(f32[2,8,128]{2,1,0:T(8,128)S(1)} %slice_reduce_fusion), channel_id=1, source_target_pairs={{0,1},{1,2},{2,3},{4,5},{5,6},{6,7},{8,9},{9,10},{10,11},{12,13},{... | collective-permute-start | bytes 24584 | tf_op jit(solution)/shard_map/ppermute | solution.py:25
  184.0 18.4 %collective-permute-start.3 = (f32[2,8,128]{2,1,0:T(8,128)S(1)}, f32[2,8,128]{2,1,0:T(8,128)S(1)}, u32[]{:S(2)}, u32[]{:S(2)}) collective-permute-start(f32[2,8,128]{2,1,0:T(8,128)S(1)} %slice_reduce_fusion), channel_id=1, source_target_pairs={{0,2},{1,3},{4,6},{5,7},{8,10},{9,11},{12,14},{13,15},{16,18},{17,... | collective-permute-start | bytes 24584 | tf_op jit(solution)/shard_map/ppermute | solution.py:25
Sparse Core Ops, SparseCore 0:
  11.5 105.9 all-gather.1
  242.2 15.7 reduce-scatter.1

commit v2 on v1

--- a/solution.py
+++ b/solution.py
@@ -10,19 +10,11 @@
 ATTEND_DIM = 64
 PAIR = 128
 CHUNK = 128
-SAFE = -60.0
 eps = 1e-05
 f32 = jnp.float32
 bf16 = jnp.bfloat16
-HIGHEST = lax.Precision.HIGHEST
 CONTRACT_ROWS = (((0,), (0,)), ((), ()))
 CONTRACT_LANES = (((1,), (1,)), ((), ()))
-
-
-def from_behind(value, axis, by):
-    peers = lax.axis_size(axis)
-    pairs = [(i, i + by) for i in range(peers) if 0 <= i + by < peers]
-    return lax.ppermute(value, axis, pairs)
 
 
 def split_two(value):
@@ -307,180 +299,333 @@
     )(x, last, perm, gain, blend, left, weights)
 
 
-def earlier(size):
-    t = lax.broadcasted_iota(jnp.int32, (size, size), 0)
-    s = lax.broadcasted_iota(jnp.int32, (size, size), 1)
-    return t > s
-
-
 def same_head():
     c = lax.broadcasted_iota(jnp.int32, (PAIR, PAIR), 0) // ATTEND_DIM
     v = lax.broadcasted_iota(jnp.int32, (PAIR, PAIR), 1) // ATTEND_DIM
     return c == v
 
 
-def sum_before(decays):
-    ones = earlier(decays.shape[0]).astype(f32).astype(bf16)
-    high, low = split_two(decays)
-    return dot32(ones, high) + dot32(ones, low)
-
-
-def sum_after(decays):
-    ones = earlier(decays.shape[0]).astype(f32).astype(bf16)
-    high, low = split_two(decays)
-    return dot32(ones, high, CONTRACT_ROWS) + dot32(ones, low, CONTRACT_ROWS)
-
-
-def column_total(decays):
-    high, low = split_two(decays)
-    ones = jnp.ones((decays.shape[0], PAIR), bf16)
-    return dot32(high, ones, CONTRACT_ROWS) + dot32(low, ones, CONTRACT_ROWS)
-
-
-def state_kernel(span, valid_ref, lora_ref, right_ref, speed_ref, k_ref, v_ref, w_ref, l_ref, t_ref):
-    rows = k_ref.shape[0]
-    valid = valid_ref[:, 0:1]
-    log_decay = -speed_ref[...] * jnp.exp(dot32(lora_ref[...], right_ref[...])) * valid
-    w_ref[...] = log_decay
+LEVELS = 7
+QUAD = 256
+OUT_CUTS = (0, 384, 768, 1024)
+
+
+def windows():
+    t = lax.broadcasted_iota(jnp.int32, (CHUNK, QUAD), 0)
+    s = lax.broadcasted_iota(jnp.int32, (CHUNK, QUAD), 1) % CHUNK
+    chosen = [s < t, s > t]
+    for level in range(LEVELS):
+        middle = (((t >> (level + 1)) << 1) + 1) << level
+        late = ((s >= middle) & (s < t)) & (t >= middle)
+        early = ((s > t) & (s < middle)) & (t < middle)
+        chosen.append(late | early)
+    return [jnp.where(c, 1.0, 0.0).astype(bf16) for c in chosen]
+
+
+def halves(values):
+    first_head = lax.broadcasted_iota(jnp.int32, (1, PAIR), 1) < ATTEND_DIM
+    return jnp.concatenate(
+        [jnp.where(first_head, values, 0.0), jnp.where(first_head, 0.0, values)], axis=0
+    ).astype(bf16)
+
+
+def mixer_kernel(
+    rkv_ref, lora_ref, right_ref, speed_ref, reward_ref, scale_ref, valid_ref, x_ref, w_ref,
+    out_ref, state_ref,
+    slots0, slots1, slots2, sums, level_of, decays, faded, y_buf, normed, expo,
+    own_state, own_total, far_state, far_total, outgoing, incoming, residual,
+    load_sem, send, recv, state_send, state_recv, total_send, total_recv, part_send, part_recv,
+):
+    rows, width = y_buf.shape
+    reqs = own_state.shape[0]
+    span = rows // reqs
+    at = position()
+    core = lax.axis_index("tensor")
+    partner = (1 - core, lax.axis_index("req"), at["y"])
+    share = x_ref.shape[1] // 2
+    load = pltpu.make_async_copy(
+        x_ref.at[:, pl.ds(pl.multiple_of(core * share, share), share)], residual, load_sem
+    )
+    load.start()
+    half = w_ref.shape[0] // 2
+    parts = (slice(0, half), slice(half, 2 * half))
+    slots = (slots0, slots1, slots2)
+    rings = []
+    for i in range(3):
+        slots[i][at["x"], at["z"], at["y"]] = w_ref[:, OUT_CUTS[i] : OUT_CUTS[i + 1]]
+        rings.append(Ring(slots[i], ORDERS[i], ("x", "z", "y"), send.at[i], recv.at[i], parts))
+    far_state[...] = jnp.zeros_like(far_state)
+    far_total[...] = jnp.zeros_like(far_total)
+
+    barrier = pltpu.get_barrier_semaphore()
+    friends = [device(moved(at, axis, by)) for axis in "xyz" for by in (1, -1)]
+    for friend in friends + [device(moved(at, "y", 2)), partner]:
+        pl.semaphore_signal(barrier, inc=1, device_id=friend, device_id_type=MESH)
+    pl.semaphore_wait(barrier, 8)
+    for ring in rings:
+        ring.start(0, 0)
+
+    for i, window in enumerate(windows()):
+        sums[i] = window
+    t = lax.broadcasted_iota(jnp.int32, (CHUNK, QUAD), 0)
+    s = lax.broadcasted_iota(jnp.int32, (CHUNK, QUAD), 1) % CHUNK
+    level = jnp.full((CHUNK, QUAD), LEVELS, jnp.int32)
+    for i in range(LEVELS):
+        level = jnp.where(((t >> i) == (s >> i) + 1) & (((t >> i) & 1) == 1), i, level)
+    level_of[...] = level
     keep = same_head()
-    for b in range(rows // span):
-        at = slice(b * span, (b + 1) * span)
-        part = log_decay[at]
-        left_over = jnp.exp(sum_after(part))
-        key = (k_ref[at].astype(f32) * valid[at] * left_over).astype(bf16)
-        state = dot32(key, v_ref[at], CONTRACT_ROWS)
-        l_ref[b, 0] = jnp.where(keep, state, 0.0).astype(l_ref.dtype)
-        t_ref[b, 0] = column_total(part)
-
-
-def local_states(valid, lora, right, speed, k, v, span):
-    rows, width = k.shape
-    pairs, reqs = width // PAIR, rows // span
-    column = pl.BlockSpec((rows, PAIR), lambda i: (0, i))
-    whole = lambda shape: pl.BlockSpec(shape, lambda i: (0,) * len(shape))
-    piece = pl.BlockSpec((reqs, 1, PAIR, PAIR), lambda i: (0, i, 0, 0))
+    ones = jnp.where(keep, 1.0, 0.0).astype(bf16)
+    head_sum = jnp.concatenate([ones, ones], axis=0)
+    first_head = lax.broadcasted_iota(jnp.int32, (1, PAIR), 1) < ATTEND_DIM
+
+    def over_head(values):
+        return dot32(jnp.concatenate(split_two(values), axis=1), head_sum)
+
+    def prepare(q, _):
+        lanes = pl.ds(pl.multiple_of(q * QUAD, QUAD), QUAD)
+        valid = valid_ref[:, 0:1]
+        rate = jnp.exp(dot32(lora_ref[...], right_ref[:, lanes]))
+        decays[:, lanes] = -speed_ref[:, lanes] * rate * valid
+        for b in range(reqs):
+            before, after, total = [], [], []
+            for c in range(span // CHUNK):
+                rows_c = slice(b * span + c * CHUNK, b * span + (c + 1) * CHUNK)
+                w = decays[rows_c, lanes]
+                both = jnp.concatenate(split_two(w), axis=0)
+                before.append(dot32(sums[0], both))
+                after.append(dot32(sums[1], both))
+                total.append(before[c][CHUNK - 1 :] + w[CHUNK - 1 :])
+            own_total[b : b + 1, lanes] = total[0] + total[1]
+            at0 = slice(b * span, b * span + CHUNK)
+            at1 = slice(b * span + CHUNK, (b + 1) * span)
+            whole = slice(b * span, (b + 1) * span)
+            r0, r1 = rkv_ref[0, at0, lanes].astype(f32), rkv_ref[0, at1, lanes].astype(f32)
+            k0 = rkv_ref[1, at0, lanes].astype(f32) * valid[at0]
+            k1 = rkv_ref[1, at1, lanes].astype(f32) * valid[at1]
+            faded[at0, lanes] = (r0 * jnp.exp(before[0])).astype(bf16)
+            faded[at1, lanes] = (r1 * jnp.exp(before[1] + total[0])).astype(bf16)
+            query1 = (r1 * jnp.exp(before[1])).astype(bf16)
+            key0 = (k0 * jnp.exp(after[0])).astype(bf16)
+            keys = jnp.concatenate(
+                [(k0 * jnp.exp(after[0] + total[1])).astype(bf16), (k1 * jnp.exp(after[1])).astype(bf16)],
+                axis=0,
+            )
+            value = rkv_ref[2, whole, lanes]
+            bonus0 = r0 * k0 * reward_ref[:, lanes]
+            bonus1 = r1 * k1 * reward_ref[:, lanes]
+            for p in range(2):
+                pair = slice(p * PAIR, (p + 1) * PAIR)
+                here = pl.ds(pl.multiple_of(q * QUAD + p * PAIR, PAIR), PAIR)
+                grown = dot32(value[:, pair], keys[:, pair], CONTRACT_ROWS)
+                own_state[b, 2 * q + p] = jnp.where(
+                    first_head, grown[:ATTEND_DIM], grown[ATTEND_DIM:]
+                ).astype(bf16)
+                grown0 = dot32(value[:CHUNK, pair], key0[:, pair], CONTRACT_ROWS)
+                grown0 = jnp.where(keep, grown0, 0.0).astype(bf16)
+                y_buf[at0, here] = over_head(bonus0[:, pair]) * value[:CHUNK, pair].astype(f32)
+                y_buf[at1, here] = over_head(bonus1[:, pair]) * value[CHUNK:, pair].astype(
+                    f32
+                ) + dot32(query1[:, pair], grown0, CONTRACT_LANES)
+
+        @pl.when(q == 0)
+        def _():
+            for ring in rings:
+                ring.arrived(0, 0)
+                ring.start(0, 1)
+
+        @pl.when(q == 1)
+        def _():
+            for ring in rings:
+                ring.arrived(0, 1)
+                ring.start(1, 0)
+
+        @pl.when(q == 2)
+        def _():
+            for ring in rings:
+                ring.arrived(1, 0)
+                ring.start(1, 1)
+
+        @pl.when(q == 3)
+        def _():
+            for ring in rings:
+                ring.arrived(1, 1)
+                ring.start(2, 0)
+
+        return 0
+
+    lax.fori_loop(0, width // QUAD, prepare, 0)
+
+    def hand_on(by):
+        to = device(moved(at, "y", by))
+        return [
+            pltpu.make_async_remote_copy(
+                own, far.at[by - 1], s_sem.at[by - 1], r_sem.at[by - 1],
+                device_id=to, device_id_type=MESH,
+            )
+            for own, far, s_sem, r_sem in (
+                (own_state, far_state, state_send, state_recv),
+                (own_total, far_total, total_send, total_recv),
+            )
+        ]
+
+    for by in range(1, SIDE):
+        @pl.when(at["y"] + by < SIDE)
+        def _():
+            for copy in hand_on(by):
+                copy.start()
+
+    def within(i, _):
+        q, c = i // 4, i % 4
+        lanes = pl.ds(pl.multiple_of(q * QUAD, QUAD), QUAD)
+        rows_c = pl.ds(pl.multiple_of(c * CHUNK, CHUNK), CHUNK)
+        both = jnp.concatenate(split_two(decays[rows_c, lanes]), axis=0)
+        for n in range(LEVELS):
+            expo[n] = dot32(sums[2 + n], both)
+        row = lax.broadcasted_iota(jnp.int32, (CHUNK, 1), 0)
+        valid = valid_ref[rows_c, 0:1]
+        for p in range(2):
+            pair = slice(p * PAIR, (p + 1) * PAIR)
+            here = pl.ds(pl.multiple_of(q * QUAD + p * PAIR, PAIR), PAIR)
+            r = rkv_ref[0, rows_c, here].astype(f32)
+            k = rkv_ref[1, rows_c, here].astype(f32) * valid
+            scores = jnp.zeros((CHUNK, QUAD), f32)
+            for n in range(LEVELS):
+                side = jnp.where(((row >> n) & 1) == 1, r, k) * jnp.exp(expo[n, :, pair])
+                found = dot32(side.astype(bf16), halves(side), CONTRACT_LANES)
+                scores = jnp.where(level_of[...] == n, found, scores)
+            values = halves(rkv_ref[2, rows_c, here].astype(f32))
+            y_buf[rows_c, here] += dot32(scores.astype(bf16), values)
+
+        @pl.when(i == 10)
+        def _():
+            for ring in rings:
+                ring.arrived(2, 0)
+                ring.start(2, 1)
+
+        return 0
+
+    lax.fori_loop(0, width // QUAD * (rows // CHUNK), within, 0)
+
+    for by in range(1, SIDE):
+        @pl.when(at["y"] >= by)
+        def _():
+            for copy in hand_on(by):
+                copy.wait_recv()
+
+    def finish(p, _):
+        here = pl.ds(pl.multiple_of(p * PAIR, PAIR), PAIR)
+        for b in range(reqs):
+            whole = slice(b * span, (b + 1) * span)
+            near = far_total[0, b : b + 1, here]
+            state = (
+                far_state[0, b, p].astype(f32)
+                + jnp.exp(near) * far_state[1, b, p].astype(f32)
+                + jnp.exp(near + far_total[1, b : b + 1, here]) * far_state[2, b, p].astype(f32)
+            )
+            final = jnp.exp(own_total[b : b + 1, here]) * state + own_state[b, p].astype(f32)
+            state_ref[b, p] = final.T
+            y = y_buf[whole, here] + dot32(faded[whole, here], halves(state), CONTRACT_LANES)
+            centred = y - over_head(y) * (1.0 / ATTEND_DIM)
+            spread = over_head(centred * centred) * (1.0 / ATTEND_DIM)
+            scaled = centred * lax.rsqrt(spread + eps) * scale_ref[:, here]
+            normed[whole, here] = (scaled * valid_ref[whole, 0:1]).astype(bf16)
+        return 0
+
+    lax.fori_loop(0, width // PAIR, finish, 0)
+    for ring in rings:
+        ring.arrived(2, 1)
+
+    def terms(side, j):
+        product = None
+        for i in range(3):
+            weight = slots[i][2 * side + j // SIDE, j % SIDE]
+            weight = weight.reshape(SIDE * weight.shape[1], weight.shape[2])
+            part = dot32(normed[:, OUT_CUTS[i] : OUT_CUTS[i + 1]], weight, CONTRACT_LANES)
+            product = part if product is None else product + part
+        return product.astype(bf16)
+
+    def exchange(j):
+        return pltpu.make_async_remote_copy(
+            outgoing.at[j], incoming.at[j], part_send.at[j], part_recv.at[j],
+            device_id=partner, device_id_type=MESH,
+        )
+
+    def give(j, _):
+        outgoing[j] = terms(1 - core, j)
+        exchange(j).start()
+        return 0
+
+    lax.fori_loop(0, 8, give, 0)
+    load.wait()
+
+    def keep_own(j, _):
+        here = pl.ds(pl.multiple_of(j * QUAD, QUAD), QUAD)
+        mine = terms(core, j).astype(f32)
+        exchange(j).wait_recv()
+        summed = mine + incoming[j].astype(f32)
+        out_ref[:, here] = (residual[:, here].astype(f32) + summed).astype(bf16)
+        return 0
+
+    lax.fori_loop(0, 8, keep_own, 0)
+
+    def sent(j, _):
+        exchange(j).wait_send()
+        return 0
+
+    lax.fori_loop(0, 8, sent, 0)
+    for by in range(1, SIDE):
+        @pl.when(at["y"] + by < SIDE)
+        def _():
+            for copy in hand_on(by):
+                copy.wait_send()
+    for ring in rings:
+        ring.finish()
+
+
+def mixer(rkv, lora, right, speed, reward, scale, valid, x, weight, reqs):
+    rows, width = rkv.shape[1:]
+    share = x.shape[1] // 2
+    pairs = width // PAIR
+    vmem = pl.BlockSpec(memory_space=pltpu.VMEM)
+    dma = pltpu.SemaphoreType.DMA
     return pl.pallas_call(
-        functools.partial(state_kernel, span),
-        grid=(pairs,),
-        in_specs=[
-            whole(valid.shape), whole(lora.shape),
-            pl.BlockSpec((right.shape[0], PAIR), lambda i: (0, i)),
-            pl.BlockSpec((1, PAIR), lambda i: (0, i)),
-            column, column,
+        mixer_kernel,
+        in_specs=[vmem] * 7 + [pl.BlockSpec(memory_space=pl.ANY), vmem],
+        out_specs=[vmem, vmem],
+        out_shape=[
+            jax.ShapeDtypeStruct((rows, share), bf16),
+            jax.ShapeDtypeStruct((reqs, pairs, PAIR, ATTEND_DIM), f32),
         ],
-        out_specs=[column, piece, piece],
-        out_shape=[
-            jax.ShapeDtypeStruct((rows, width), f32),
-            jax.ShapeDtypeStruct((reqs, pairs, PAIR, PAIR), bf16),
-            jax.ShapeDtypeStruct((reqs, pairs, PAIR, PAIR), f32),
+        scratch_shapes=[
+            *(
+                pltpu.VMEM((SIDE, SIDE, SIDE, weight.shape[0], OUT_CUTS[i + 1] - OUT_CUTS[i]), bf16)
+                for i in range(3)
+            ),
+            pltpu.VMEM((2 + LEVELS, CHUNK, QUAD), bf16),
+            pltpu.VMEM((CHUNK, QUAD), jnp.int32),
+            pltpu.VMEM((rows, width), f32),
+            pltpu.VMEM((rows, width), bf16),
+            pltpu.VMEM((rows, width), f32),
+            pltpu.VMEM((rows, width), bf16),
+            pltpu.VMEM((LEVELS, CHUNK, QUAD), f32),
+            pltpu.VMEM((reqs, pairs, ATTEND_DIM, PAIR), bf16),
+            pltpu.VMEM((reqs, width), f32),
+            pltpu.VMEM((3, reqs, pairs, ATTEND_DIM, PAIR), bf16),
+            pltpu.VMEM((3, reqs, width), f32),
+            pltpu.VMEM((8, rows, QUAD), bf16),
+            pltpu.VMEM((8, rows, QUAD), bf16),
+            pltpu.VMEM((rows, share), bf16),
+            dma,
+            dma((3, 3, 4)), dma((3, 3, 4)),
+            dma((3,)), dma((3,)), dma((3,)), dma((3,)),
+            dma((8,)), dma((8,)),
         ],
-        compiler_params=pltpu.CompilerParams(vmem_limit_bytes=32 << 20),
-        cost_estimate=pl.CostEstimate(flops=10**9, bytes_accessed=8 << 20, transcendentals=10**6),
-        name="local_states",
-    )(valid, lora, right, speed, k, v)
-
-
-def within_chunk_stepwise(r, k, v, w):
-    rows = lax.broadcasted_iota(jnp.int32, (CHUNK, 1), 0)
-    ones = jnp.ones((CHUNK, PAIR), f32)
-    keep = same_head()
-
-    def token(t, carried):
-        state, out = carried
-        mine = rows == t
-        dot = functools.partial(lax.dot_general, precision=HIGHEST, preferred_element_type=f32)
-        out = out + dot(jnp.where(mine, r, 0.0), state, (((1,), (0,)), ((), ())))
-        fade = jnp.exp(dot(jnp.where(mine, w, 0.0), ones, CONTRACT_ROWS))
-        dyad = jnp.where(keep, dot(jnp.where(mine, k, 0.0), v, CONTRACT_ROWS), 0.0)
-        return fade * state + dyad, out
-
-    zero = jnp.zeros((PAIR, PAIR), f32)
-    return lax.fori_loop(0, CHUNK, token, (zero, jnp.zeros((CHUNK, PAIR), f32)))[1]
-
-
-def read_kernel(
-    span, valid_ref, r_ref, k_ref, v_ref, w_ref, in_ref, l_ref, t_ref, reward_ref, scale_ref,
-    out_ref, state_ref, inner,
-):
-    rows = k_ref.shape[0]
-    keep = same_head()
-    average = jnp.where(keep, 1.0, 0.0).astype(bf16)
-    first_head = lax.broadcasted_iota(jnp.int32, (1, PAIR), 1) < ATTEND_DIM
-    strict = earlier(CHUNK)
-    strict = jnp.concatenate([strict, strict], axis=1)
-    for b in range(rows // span):
-        state = in_ref[b, 0]
-        final = jnp.exp(t_ref[b, 0]) * state + l_ref[b, 0].astype(f32)
-        state_ref[b, 0, 0] = final[:ATTEND_DIM, :ATTEND_DIM]
-        state_ref[b, 0, 1] = final[ATTEND_DIM:, ATTEND_DIM:]
-        for c in range(span // CHUNK):
-            at = slice(b * span + c * CHUNK, b * span + (c + 1) * CHUNK)
-            valid = valid_ref[at, 0:1]
-            r, v = r_ref[at].astype(f32), v_ref[at]
-            k = k_ref[at].astype(f32) * valid
-            w = w_ref[at]
-            before = sum_before(w)
-            cum = before + w
-            mid, last = before[CHUNK // 2 : CHUNK // 2 + 1], cum[CHUNK - 1 :]
-            gentle = jnp.min(jnp.minimum(mid, last - mid)) > SAFE
-
-            @pl.when(gentle)
-            def _():
-                query = (r * jnp.exp(before - mid)).astype(bf16)
-                key = k * jnp.exp(mid - cum)
-                keys = jnp.concatenate(
-                    [jnp.where(first_head, key, 0.0), jnp.where(first_head, 0.0, key)], axis=0
-                ).astype(bf16)
-                scores = jnp.where(strict, dot32(query, keys, CONTRACT_LANES), 0.0).astype(bf16)
-                value = v.astype(f32)
-                values = jnp.concatenate(
-                    [jnp.where(first_head, value, 0.0), jnp.where(first_head, 0.0, value)], axis=0
-                ).astype(bf16)
-                inner[...] = dot32(scores, values)
-
-            @pl.when(jnp.logical_not(gentle))
-            def _():
-                inner[...] = within_chunk_stepwise(r, k, v.astype(f32), w)
-
-            high, low = split_two(r * reward_ref[...] * k)
-            own = (dot32(high, average) + dot32(low, average)) * v.astype(f32)
-            y = inner[...] + own + dot32((r * jnp.exp(before)).astype(bf16), state.astype(bf16))
-            if c + 1 < span // CHUNK:
-                left_over = (k * jnp.exp(sum_after(w))).astype(bf16)
-                grown = dot32(left_over, v, CONTRACT_ROWS)
-                state = jnp.exp(column_total(w)) * state + jnp.where(keep, grown, 0.0)
-            high, low = split_two(y)
-            centred = y - (dot32(high, average) + dot32(low, average)) * (1.0 / ATTEND_DIM)
-            high, low = split_two(centred * centred)
-            spread = (dot32(high, average) + dot32(low, average)) * (1.0 / ATTEND_DIM)
-            normed = centred * lax.rsqrt(spread + eps) * scale_ref[...] * valid
-            out_ref[at] = normed.astype(bf16)
-
-
-def read_states(valid, r, k, v, w, incoming, local_state, totals, reward, scale, span):
-    rows, width = k.shape
-    pairs, reqs = width // PAIR, rows // span
-    column = pl.BlockSpec((rows, PAIR), lambda i: (0, i))
-    line = pl.BlockSpec((1, PAIR), lambda i: (0, i))
-    piece = pl.BlockSpec((reqs, 1, PAIR, PAIR), lambda i: (0, i, 0, 0))
-    heads = pl.BlockSpec((reqs, 1, 2, ATTEND_DIM, ATTEND_DIM), lambda i: (0, i, 0, 0, 0))
-    return pl.pallas_call(
-        functools.partial(read_kernel, span),
-        grid=(pairs,),
-        in_specs=[
-            pl.BlockSpec(valid.shape, lambda i: (0, 0)),
-            column, column, column, column, piece, piece, piece, line, line,
-        ],
-        out_specs=[column, heads],
-        out_shape=[
-            jax.ShapeDtypeStruct((rows, width), bf16),
-            jax.ShapeDtypeStruct((reqs, pairs, 2, ATTEND_DIM, ATTEND_DIM), f32),
-        ],
-        scratch_shapes=[pltpu.VMEM((CHUNK, PAIR), f32)],
-        compiler_params=pltpu.CompilerParams(vmem_limit_bytes=32 << 20),
-        cost_estimate=pl.CostEstimate(flops=2 * 10**9, bytes_accessed=8 << 20, transcendentals=10**6),
-        name="read_states",
-    )(valid, r, k, v, w, incoming, local_state, totals, reward, scale)
+        compiler_params=pltpu.CompilerParams(
+            collective_id=1, has_side_effects=True, vmem_limit_bytes=56 << 20
+        ),
+        cost_estimate=pl.CostEstimate(flops=40 * 10**9, bytes_accessed=32 << 20, transcendentals=0),
+        name="mixer",
+    )(rkv, lora, right, speed, reward, scale, valid, x, weight)
 
 
 def local(
@@ -501,9 +646,7 @@
     rows = reqs * span
     local_width = feature_fading_speed.shape[0]
     x = incoming_activations.reshape(rows, width)
-    weight_out = lax.all_gather(
-        learner_projection_slices.T.astype(bf16), ("req", "seq"), axis=0, tiled=True
-    )
+    weight_out = learner_projection_slices.T.astype(bf16)
     positions = lax.axis_index("seq") * span + jnp.arange(span, dtype=jnp.int32)
     valid = (positions[None, :] < prompt_extents[:, None]).astype(f32).reshape(rows, 1)
     valid = jnp.broadcast_to(valid, (rows, PAIR))
@@ -514,31 +657,12 @@
         standardize_scaling[None], lagged_blending_weights, fading_left_matrix,
         learner_acceptor_lookup_slices,
     )
-    r, k, v = projected
-    decays, states, totals = local_states(
-        valid, lora, fading_right_matrix, feature_fading_speed[None], k, v, span
-    )
-    incoming = jnp.zeros(states.shape, f32)
-    sent = jnp.zeros_like(totals)
-    for by in range(1, lax.axis_size("seq")):
-        far_state = from_behind(states, "seq", by).astype(f32)
-        incoming = incoming + jnp.exp(sent) * far_state
-        if by + 1 < lax.axis_size("seq"):
-            far_total = from_behind(totals[..., 0], "seq", by)
-            sent = sent + far_total[..., None]
-    normed, final = read_states(
-        valid, r, k, v, decays, incoming, states, totals,
-        self_reward[None], cluster_scaling_vector[None], span,
+    hidden, final = mixer(
+        projected, lora, fading_right_matrix, feature_fading_speed[None], self_reward[None],
+        cluster_scaling_vector[None], valid, x, weight_out, reqs,
     )
     stretch_states = final.reshape(reqs, 1, local_width // ATTEND_DIM, ATTEND_DIM * ATTEND_DIM)
-    terms = dot32(normed, weight_out, CONTRACT_LANES)
-    summed = lax.psum_scatter(
-        terms.astype(bf16), "tensor", scatter_dimension=1, tiled=True
-    ).astype(f32)
-    share = width // lax.axis_size("tensor")
-    residual = lax.dynamic_slice_in_dim(x, lax.axis_index("tensor") * share, share, 1)
-    hidden_out = (residual.astype(f32) + summed).astype(bf16).reshape(reqs, span, share)
-    return (hidden_out, stretch_states)
+    return (hidden.reshape(reqs, span, hidden.shape[1]), stretch_states)
 
 
 def solution(mesh):

time: 271 us -> 201 us (0.74)
  waiting for transfers between devices: 31.7 us -> 0 us
  between operations: 14.3 us -> 0.67 us
  matrix products: 9.48 us -> 0 us
  starting transfers between devices: 8.77 us -> 0 us
  other arithmetic: 7.51 us -> 2.35 us
  Pallas kernels: 191 us -> 188 us
    pallas_call x1, Pallas kernels: 152 us -> 123 us  [project(): pl.pallas_call(project_kernel, in_specs=[pl.BlockSpec(memory_space=pl.ANY...]
    pallas_call x2 -> x1, Pallas kernels: 38.2 us -> 64.8 us  [mixer(): pl.pallas_call(mixer_kernel, in_specs=[vmem] * 7 + [pl.BlockSpec(memory_s...]
    ppermute x5 -> x0, waiting for transfers between devices: 16.9 us -> none  [from_behind(): return lax.ppermute(value, axis, pairs)]
    reduce_scatter x1 -> x0, waiting for transfers between devices: 14.7 us -> none  [local(): lax.psum_scatter(terms.astype(bf16), 'tensor', scatter_dimension=1, tiled...]
    dot_general x1 -> x0, matrix products: 9.48 us -> none  [dot32(): return lax.dot_general(a, b, dims, preferred_element_type=f32)]
    ppermute x5 -> x0, starting transfers between devices: 8.69 us -> none  [from_behind(): return lax.ppermute(value, axis, pairs)]
    convert_element_type x2 -> x1, other arithmetic: 6.06 us -> 1.62 us  [local(): weight_out = learner_projection_slices.T.astype(bf16)]
    unnamed x12 -> x3, local copies, waits for them, and re-layouts: 0.67 us -> 3.79 us
  transfers between devices with their start and end apart: 7 -> 0, of which waited for: 3 -> 0; matrix products, arithmetic and copies ran while one was open for 3% -> 0% of each run, Pallas kernels for 71% -> 0%
where the time goes in v2:
time: 201 us; the launch traced here: 200 us
  Pallas kernels  188 us (94%)
  local copies, waits for them, and re-layouts  9.43 us (5%)
  other arithmetic  2.35 us (1%)
    pallas_call x1, Pallas kernels, project(): pl.pallas_call(project_kernel, in_specs=[pl.BlockSpec(memory_space=pl.ANY...  123 us
    pallas_call x1, Pallas kernels, mixer(): pl.pallas_call(mixer_kernel, in_specs=[vmem] * 7 + [pl.BlockSpec(memory_s...  64.8 us

profile of v2, /device:TPU:16, one launch (start us, length us, event | category | flops | bytes accessed | tf_op | source)
XLA Modules:
  0.0 200.0 jit_solution(10780885006242932743)
XLA Ops:
  0.6 0.7 fusion
  1.4 0.8 reshape.43
  2.2 0.7 reshape.44.perm_ref
  2.9 0.9 slice.3
  3.8 0.6 copy.22
  4.4 1.6 convert_bitcast_fusion.w_ref
  6.1 0.8 broadcast_in_dim.23.valid_ref
  6.9 122.8 %project.1 = (bf16[3,512,1024]{2,1,0:T(8,128)(2,1)}, bf16[512,128]{1,0:T(8,128)(2,1)}) custom-call(bf16[512,4096]{1,0:T(8,128)(2,1)} %bitcast.23, bf16[2,4096]{1,0:T(2,128)(2,1)} %bitcast.21, s32[1,4096]{1,0:T(1,128)} %reshape.44.perm_ref, f32[1,4096]{1,0:T(1,128)} %bitcast.25, f32[4,4096]{1,0:T(4,128)} %blend_ref.1, bf16[4096,128]{1,0:T(8,128)(2,1)} %left_ref.1, ...), custom_call_target="tpu_custom_call" | custom-call | flops 99999997952 | bytes 33554432 | tf_op jit(solution)/shard_map/project/pallas_call | solution.py:269
  129.7 64.8 %mixer.1 = (bf16[512,2048]{1,0:T(8,128)(2,1)}, f32[2,8,128,64]{3,2,1,0:T(8,128)}) custom-call(bf16[3,512,1024]{2,1,0:T(8,128)(2,1)} %get-tuple-element.6.rkv_ref, bf16[512,128]{1,0:T(8,128)(2,1)} %get-tuple-element.7.lora_ref, bf16[128,1024]{1,0:T(8,128)(2,1)} %right_ref.1, f32[1,1024]{1,0:T(1,128)} %bitcast.26, f32[1,1024]{1,0:T(1,128)} %bitcast.27, ...), custom_call_target="tpu_custom_call" | custom-call | flops 40000000000 | bytes 33554432 | tf_op jit(solution)/shard_map/mixer/pallas_call | solution.py:591
  194.5 2.4 %reshape.46 = f32[2,1,16,4096]{3,2,0,1:T(8,128)} reshape(f32[2,8,128,64]{3,2,1,0:T(8,128)} %get-tuple-element.9) | data formatting | bytes 1048576 | tf_op jit(solution)/shard_map/reshape | solution.py:664
  196.9 3.2 %copy.24 = bf16[2,256,2048]{2,1,0:T(8,128)(2,1)} copy(bf16[2,256,2048]{2,1,0:T(8,128)(2,1)} %bitcast.18) | data formatting | bytes 4194304
  (3 shorter events, 0.0 us)

commit v3 on v2

--- a/solution.py
+++ b/solution.py
@@ -32,6 +32,7 @@
 PLACES = (("z", "y", "x"), ("x", "y", "z"), ("y", "x", "z"))
 SIDE = 4
 STEP = 512
+OUT_CUTS = (0, 384, 768, 1024)
 
 
 def position():
@@ -70,41 +71,58 @@
             index.append(slice(None) if turn < phase else where if turn == phase else self.at[axis])
         return self.slots.at[(*index, *part)]
 
-    def copy(self, phase, kind, right):
+    def copy(self, phase, slot):
         axis = self.order[phase]
-        to = moved(self.at, axis, 1 if right else -1)
-        if kind == 0:
-            ref = self.block(phase, self.at[axis], ())
-        else:
-            source = moved(self.at, axis, -1 if right else 1)[axis]
-            ref = self.block(phase, source, (self.parts[0 if right else 1],))
-        slot = 2 * kind + (0 if right else 1)
+        right = slot in (0, 2, 4)
+        part = 0 if slot in (0, 3, 4) else 1
+        by = 1 if right else -1
+        source = self.at if slot < 4 else moved(self.at, axis, -by)
+        ref = self.block(phase, source[axis], (self.parts[part],))
         return pltpu.make_async_remote_copy(
             ref, ref, self.send.at[phase, slot], self.recv.at[phase, slot],
-            device_id=device(to), device_id_type=MESH,
+            device_id=device(moved(self.at, axis, by)), device_id_type=MESH,
         )
 
-    def start(self, phase, kind):
-        for right in (True, False):
-            self.copy(phase, kind, right).start()
-
-    def arrived(self, phase, kind):
-        for right in (True, False):
-            self.copy(phase, kind, right).wait_recv()
-
-    def finish(self):
-        for phase in range(3):
-            for kind in range(2):
-                for right in (True, False):
-                    self.copy(phase, kind, right).wait_send()
+    def start(self, phase):
+        for slot in range(4):
+            self.copy(phase, slot).start()
+
+    def turn(self, phase):
+        for slot in range(2):
+            self.copy(phase, slot).wait_recv()
+            self.copy(phase, slot + 4).start()
+
+    def near(self, phase):
+        for slot in range(2, 4):
+            self.copy(phase, slot).wait_recv()
+
+    def far(self, phase):
+        for slot in range(4, 6):
+            self.copy(phase, slot).wait_recv()
+
+    def settle(self, phase):
+        self.near(phase)
+        self.far(phase)
+
+    def sent(self, phase):
+        for slot in range(6):
+            self.copy(phase, slot).wait_send()
+
+
+def each(rings, *steps):
+    for name, phase in steps:
+        for ring in rings:
+            getattr(ring, name)(phase)
 
 
 def project_kernel(
-    x_ref, last_ref, perm_ref, gain_ref, blend_ref, left_ref, w_ref, out_ref, lora_ref,
-    slots, stack, mixed, chosen, picked, total, stats, low_rank, tail, load_sem, tail_sem, send, recv,
+    x_ref, perm_ref, gain_ref, blend_ref, left_ref, w_ref, w_out_ref,
+    out_ref, lora_ref, plane0, plane1, plane2,
+    slots, slots0, slots1, slots2, stack, mixed, chosen, picked, total, stats, low_rank, last, tail,
+    load_sem, save_sem, tail_sem, send, recv, out_send, out_recv,
 ):
     rows, width = x_ref.shape
-    reqs = last_ref.shape[0]
+    reqs = last.shape[0]
     span = rows // reqs
     at = position()
     half = w_ref.shape[1] // 2
@@ -117,25 +135,36 @@
     for m in range(3):
         slots[(m, *(at[axis] for axis in PLACES[m]))] = w_ref[m].astype(bf16)
     greet_neighbours(at)
+    each(rings, ("start", 0))
+    load.wait()
+    for b in range(reqs):
+        end = (b + 1) * span
+        last[b : b + 1, :] = stack[end - 16 : end, :].astype(f32)[15:16].astype(bf16)
     hand_on = pltpu.make_async_remote_copy(
-        last_ref, tail, tail_sem.at[0], tail_sem.at[1],
+        last, tail, tail_sem.at[0], tail_sem.at[1],
         device_id=device(moved(at, "y", 1)), device_id_type=MESH,
     )
     hand_on.start()
-    for ring in rings:
-        ring.start(0, 0)
+
+    out_slots = (slots0, slots1, slots2)
+    out_rings = []
+    turned = w_out_ref[...].T.astype(bf16)
+    for i in range(3):
+        places = tuple(axis for axis in "xzy" if axis != ORDERS[i][2])
+        out_slots[i][tuple(at[axis] for axis in places)] = turned[:, OUT_CUTS[i] : OUT_CUTS[i + 1]]
+        out_rings.append(Ring(out_slots[i], ORDERS[i], places, out_send.at[i], out_recv.at[i], parts))
 
     table = jnp.concatenate([gain_ref[...], blend_ref[0:3, :]], axis=0)
     first = table.astype(bf16)
     rest = table - first.astype(f32)
     second = rest.astype(bf16)
     third = (rest - second.astype(f32)).astype(bf16)
+    each(rings, ("turn", 0))
     hand_on.wait_recv()
     before = jnp.where(at["y"] > 0, tail[...].astype(f32), 0.0).astype(bf16)
     pad = jnp.zeros((16 - reqs - 12, width), bf16)
     stack[rows:, :] = jnp.concatenate([before, first, second, third, pad], axis=0)
     low_rank[...] = jnp.zeros_like(low_rank)
-    load.wait()
 
     def row_stats(i, _):
         here = pl.ds(pl.multiple_of(i * 16, 16), 16)
@@ -148,6 +177,7 @@
         return 0
 
     lax.fori_loop(0, stack.shape[0] // 16, row_stats, 0)
+    each(rings, ("settle", 0), ("start", 1))
 
     def shifted(values, gain):
         mean, scale = stats[0, :, 0:1], stats[1, :, 0:1]
@@ -164,7 +194,21 @@
 
     def mix_step(step, _):
         here = pl.ds(pl.multiple_of(step * STEP, STEP), STEP)
-        names = perm_ref[:, here]
+        y, x0 = step // 2, (step % 2) * 2
+        names = []
+        for i in range(2):
+            for z in range(0, SIDE, 2):
+                at_row = (x0 + i) * 8 + z * 2 + y // 2
+                low, high = perm_ref[pl.ds(at_row, 1), :], perm_ref[pl.ds(at_row + 2, 1), :]
+                low_up, high_up = pltpu.roll(low, 64, axis=1), pltpu.roll(high, 64, axis=1)
+                even = y % 2 == 0
+                names.append(
+                    jnp.where(
+                        lax.broadcasted_iota(jnp.int32, (1, 128), 1) < 64,
+                        jnp.where(even, low, low_up), jnp.where(even, high_up, high),
+                    )
+                )
+        names = jnp.concatenate(names, axis=1)
         picked[...] = jnp.zeros_like(picked)
 
         def pick(d, _):
@@ -180,7 +224,6 @@
             return 0
 
         lax.fori_loop(0, width // depth, pick, 0)
-        y, x0 = step // 2, (step % 2) * 2
         for i in range(2):
             values = picked[:, i * piece : (i + 1) * piece]
             own = values[rows + reqs :]
@@ -201,29 +244,18 @@
             left_ref[pl.ds(pl.multiple_of(step * STEP, STEP), STEP), :],
         )
 
-        @pl.when(step == 0)
-        def _():
-            for ring in rings:
-                ring.arrived(0, 0)
-                ring.start(0, 1)
-
-        @pl.when(step == 1)
-        def _():
-            for ring in rings:
-                ring.arrived(0, 1)
-                ring.start(1, 0)
-
-        @pl.when(step == 3)
-        def _():
-            for ring in rings:
-                ring.arrived(1, 0)
-                ring.start(1, 1)
-
-        @pl.when(step == 4)
-        def _():
-            for ring in rings:
-                ring.arrived(1, 1)
-                ring.start(2, 0)
+        for when, group, steps in (
+            (0, rings, (("turn", 1),)),
+            (2, rings, (("settle", 1), ("start", 2))),
+            (3, out_rings, (("start", 0),)),
+            (4, out_rings, (("turn", 0),)),
+            (5, out_rings, (("settle", 0), ("start", 1))),
+            (7, out_rings, (("turn", 1),)),
+            (7, rings, (("turn", 2),)),
+        ):
+            @pl.when(step == when)
+            def _():
+                each(group, *steps)
 
         return 0
 
@@ -249,45 +281,55 @@
         lax.fori_loop(0, 12, tile, 0)
 
     products(0, True)
-    for ring in rings:
-        ring.arrived(2, 0)
-        ring.start(2, 1)
+    each(rings, ("near", 2))
     products(1, False)
     products(3, False)
-    for ring in rings:
-        ring.arrived(2, 1)
+    each(out_rings, ("settle", 1))
+    saves = [
+        pltpu.make_async_copy(kept, plane, save_sem.at[i])
+        for i, (plane, kept) in enumerate(zip((plane0, plane1, plane2), out_slots))
+    ]
+    for save in saves:
+        save.start()
+    each(rings, ("far", 2))
     products(2, False)
     hand_on.wait_send()
-    for ring in rings:
-        ring.finish()
-
-
-def project(x, last, perm, gain, blend, left, weights):
+    for save in saves:
+        save.wait()
+    each(rings, ("sent", 0), ("sent", 1), ("sent", 2))
+    each(out_rings, ("sent", 0), ("sent", 1))
+
+
+def project(x, reqs, perm, gain, blend, left, weights, out_weight):
     rows, width = x.shape
+    shard = weights.shape[1]
+    cuts = [OUT_CUTS[i + 1] - OUT_CUTS[i] for i in range(3)]
+    dma = pltpu.SemaphoreType.DMA
     inner, local_width = left.shape[1], weights.shape[2]
     vmem = pl.BlockSpec(memory_space=pltpu.VMEM)
     return pl.pallas_call(
         project_kernel,
         in_specs=[pl.BlockSpec(memory_space=pl.ANY)] + [vmem] * 6,
-        out_specs=[vmem, vmem],
+        out_specs=[vmem] * 2 + [pl.BlockSpec(memory_space=pl.ANY)] * 3,
         out_shape=[
             jax.ShapeDtypeStruct((3, rows, local_width), bf16),
             jax.ShapeDtypeStruct((rows, inner), bf16),
+            *(jax.ShapeDtypeStruct((SIDE, SIDE, shard, cut), bf16) for cut in cuts),
         ],
         scratch_shapes=[
             pltpu.VMEM((3, SIDE, SIDE, SIDE, *weights.shape[1:]), bf16),
+            *(pltpu.VMEM((SIDE, SIDE, shard, cut), bf16) for cut in cuts),
             pltpu.VMEM((rows + 16, width), bf16),
             pltpu.VMEM((3, SIDE, rows, width // SIDE), bf16),
-            pltpu.VMEM((width // 2, STEP), bf16),
+            pltpu.VMEM((width // 4, STEP), bf16),
             pltpu.VMEM((rows + 16, STEP), f32),
             pltpu.VMEM((3, rows, local_width), f32),
             pltpu.VMEM((2, rows + 16, PAIR), f32),
             pltpu.VMEM((rows, inner), f32),
-            pltpu.VMEM(last.shape, bf16),
-            pltpu.SemaphoreType.DMA,
-            pltpu.SemaphoreType.DMA((2,)),
-            pltpu.SemaphoreType.DMA((3, 3, 4)),
-            pltpu.SemaphoreType.DMA((3, 3, 4)),
+            pltpu.VMEM((reqs, width), bf16),
+            pltpu.VMEM((reqs, width), bf16),
+            dma, dma((3,)), dma((2,)),
+            dma((3, 3, 6)), dma((3, 3, 6)), dma((3, 2, 6)), dma((3, 2, 6)),
         ],
         compiler_params=pltpu.CompilerParams(
             collective_id=0, has_side_effects=True, vmem_limit_bytes=61 << 20
@@ -296,7 +338,7 @@
             flops=100 * 10**9, bytes_accessed=32 << 20, transcendentals=0
         ),
         name="project",
-    )(x, last, perm, gain, blend, left, weights)
+    )(x, perm, gain, blend, left, weights, out_weight)
 
 
 def same_head():
@@ -307,7 +349,6 @@
 
 LEVELS = 7
 QUAD = 256
-OUT_CUTS = (0, 384, 768, 1024)
 
 
 def windows():
@@ -330,11 +371,12 @@
 
 
 def mixer_kernel(
-    rkv_ref, lora_ref, right_ref, speed_ref, reward_ref, scale_ref, valid_ref, x_ref, w_ref,
+    extents_ref, rkv_ref, lora_ref, right_ref, speed_ref, reward_ref, scale_ref, x_ref,
+    plane0, plane1, plane2,
     out_ref, state_ref,
-    slots0, slots1, slots2, sums, level_of, decays, faded, y_buf, normed, expo,
+    slots0, slots1, slots2, valid_ref, sums, level_of, decays, faded, y_buf, normed, expo,
     own_state, own_total, far_state, far_total, outgoing, incoming, residual,
-    load_sem, send, recv, state_send, state_recv, total_send, total_recv, part_send, part_recv,
+    load_sem, plane_sem, send, recv, state_send, state_recv, total_send, total_recv, part_send, part_recv,
 ):
     rows, width = y_buf.shape
     reqs = own_state.shape[0]
@@ -347,13 +389,17 @@
         x_ref.at[:, pl.ds(pl.multiple_of(core * share, share), share)], residual, load_sem
     )
     load.start()
-    half = w_ref.shape[0] // 2
+    half = plane0.shape[2] // 2
     parts = (slice(0, half), slice(half, 2 * half))
     slots = (slots0, slots1, slots2)
     rings = []
     for i in range(3):
-        slots[i][at["x"], at["z"], at["y"]] = w_ref[:, OUT_CUTS[i] : OUT_CUTS[i + 1]]
         rings.append(Ring(slots[i], ORDERS[i], ("x", "z", "y"), send.at[i], recv.at[i], parts))
+    fills = []
+    for i, plane in enumerate((plane0, plane1, plane2)):
+        own = rings[i].block(2, at[ORDERS[i][2]], ())
+        fills.append(pltpu.make_async_copy(plane, own, plane_sem.at[i]))
+        fills[i].start()
     far_state[...] = jnp.zeros_like(far_state)
     far_total[...] = jnp.zeros_like(far_total)
 
@@ -362,8 +408,15 @@
     for friend in friends + [device(moved(at, "y", 2)), partner]:
         pl.semaphore_signal(barrier, inc=1, device_id=friend, device_id_type=MESH)
     pl.semaphore_wait(barrier, 8)
-    for ring in rings:
-        ring.start(0, 0)
+    for fill in fills:
+        fill.wait()
+    each(rings, ("start", 2))
+    row = lax.broadcasted_iota(jnp.int32, (rows, PAIR), 0)
+    token = at["y"] * span + row % span
+    inside = jnp.zeros((rows, PAIR), f32)
+    for b in range(reqs):
+        inside = jnp.where((row // span == b) & (token < extents_ref[b]), 1.0, inside)
+    valid_ref[...] = inside
 
     for i, window in enumerate(windows()):
         sums[i] = window
@@ -427,30 +480,6 @@
                     f32
                 ) + dot32(query1[:, pair], grown0, CONTRACT_LANES)
 
-        @pl.when(q == 0)
-        def _():
-            for ring in rings:
-                ring.arrived(0, 0)
-                ring.start(0, 1)
-
-        @pl.when(q == 1)
-        def _():
-            for ring in rings:
-                ring.arrived(0, 1)
-                ring.start(1, 0)
-
-        @pl.when(q == 2)
-        def _():
-            for ring in rings:
-                ring.arrived(1, 0)
-                ring.start(1, 1)
-
-        @pl.when(q == 3)
-        def _():
-            for ring in rings:
-                ring.arrived(1, 1)
-                ring.start(2, 0)
-
         return 0
 
     lax.fori_loop(0, width // QUAD, prepare, 0)
@@ -496,11 +525,9 @@
             values = halves(rkv_ref[2, rows_c, here].astype(f32))
             y_buf[rows_c, here] += dot32(scores.astype(bf16), values)
 
-        @pl.when(i == 10)
+        @pl.when(i == 3)
         def _():
-            for ring in rings:
-                ring.arrived(2, 0)
-                ring.start(2, 1)
+            each(rings, ("turn", 2))
 
         return 0
 
@@ -532,8 +559,7 @@
         return 0
 
     lax.fori_loop(0, width // PAIR, finish, 0)
-    for ring in rings:
-        ring.arrived(2, 1)
+    each(rings, ("settle", 2))
 
     def terms(side, j):
         product = None
@@ -578,19 +604,19 @@
         def _():
             for copy in hand_on(by):
                 copy.wait_send()
-    for ring in rings:
-        ring.finish()
-
-
-def mixer(rkv, lora, right, speed, reward, scale, valid, x, weight, reqs):
+    each(rings, ("sent", 2))
+
+
+def mixer(extents, rkv, lora, right, speed, reward, scale, x, planes):
     rows, width = rkv.shape[1:]
-    share = x.shape[1] // 2
+    share, reqs, shard = x.shape[1] // 2, extents.shape[0], planes[0].shape[2]
     pairs = width // PAIR
     vmem = pl.BlockSpec(memory_space=pltpu.VMEM)
+    away = pl.BlockSpec(memory_space=pl.ANY)
     dma = pltpu.SemaphoreType.DMA
     return pl.pallas_call(
         mixer_kernel,
-        in_specs=[vmem] * 7 + [pl.BlockSpec(memory_space=pl.ANY), vmem],
+        in_specs=[pl.BlockSpec(memory_space=pltpu.SMEM)] + [vmem] * 6 + [away] * 4,
         out_specs=[vmem, vmem],
         out_shape=[
             jax.ShapeDtypeStruct((rows, share), bf16),
@@ -598,9 +624,10 @@
         ],
         scratch_shapes=[
             *(
-                pltpu.VMEM((SIDE, SIDE, SIDE, weight.shape[0], OUT_CUTS[i + 1] - OUT_CUTS[i]), bf16)
+                pltpu.VMEM((SIDE, SIDE, SIDE, shard, OUT_CUTS[i + 1] - OUT_CUTS[i]), bf16)
                 for i in range(3)
             ),
+            pltpu.VMEM((rows, PAIR), f32),
             pltpu.VMEM((2 + LEVELS, CHUNK, QUAD), bf16),
             pltpu.VMEM((CHUNK, QUAD), jnp.int32),
             pltpu.VMEM((rows, width), f32),
@@ -615,8 +642,8 @@
             pltpu.VMEM((8, rows, QUAD), bf16),
             pltpu.VMEM((8, rows, QUAD), bf16),
             pltpu.VMEM((rows, share), bf16),
-            dma,
-            dma((3, 3, 4)), dma((3, 3, 4)),
+            dma, dma((3,)),
+            dma((3, 3, 6)), dma((3, 3, 6)),
             dma((3,)), dma((3,)), dma((3,)), dma((3,)),
             dma((8,)), dma((8,)),
         ],
@@ -625,7 +652,7 @@
         ),
         cost_estimate=pl.CostEstimate(flops=40 * 10**9, bytes_accessed=32 << 20, transcendentals=0),
         name="mixer",
-    )(rkv, lora, right, speed, reward, scale, valid, x, weight)
+    )(extents, rkv, lora, right, speed, reward, scale, x, *planes)
 
 
 def local(
@@ -646,20 +673,14 @@
     rows = reqs * span
     local_width = feature_fading_speed.shape[0]
     x = incoming_activations.reshape(rows, width)
-    weight_out = learner_projection_slices.T.astype(bf16)
-    positions = lax.axis_index("seq") * span + jnp.arange(span, dtype=jnp.int32)
-    valid = (positions[None, :] < prompt_extents[:, None]).astype(f32).reshape(rows, 1)
-    valid = jnp.broadcast_to(valid, (rows, PAIR))
-    shard = learner_acceptor_lookup_slices.shape[1]
-    perm = learner_line_permutation.reshape(SIDE * SIDE, SIDE, shard).transpose(1, 0, 2)
-    projected, lora = project(
-        x, incoming_activations[:, span - 1, :], perm.reshape(1, width),
-        standardize_scaling[None], lagged_blending_weights, fading_left_matrix,
-        learner_acceptor_lookup_slices,
+    projected, lora, *planes = project(
+        x, reqs, learner_line_permutation.reshape(width // PAIR, PAIR), standardize_scaling[None],
+        lagged_blending_weights, fading_left_matrix, learner_acceptor_lookup_slices,
+        learner_projection_slices,
     )
     hidden, final = mixer(
-        projected, lora, fading_right_matrix, feature_fading_speed[None], self_reward[None],
-        cluster_scaling_vector[None], valid, x, weight_out, reqs,
+        prompt_extents, projected, lora, fading_right_matrix, feature_fading_speed[None],
+        self_reward[None], cluster_scaling_vector[None], x, planes,
     )
     stretch_states = final.reshape(reqs, 1, local_width // ATTEND_DIM, ATTEND_DIM * ATTEND_DIM)
     return (hidden.reshape(reqs, span, hidden.shape[1]), stretch_states)

time: 201 us -> 189 us (0.940)
  Pallas kernels: 188 us -> 180 us
  other arithmetic: 2.35 us -> 0 us
    pallas_call x1, Pallas kernels: 64.8 us -> 48.6 us  [mixer(): pl.pallas_call(mixer_kernel, in_specs=[pl.BlockSpec(memory_space=pltpu.SM...]
    pallas_call x1, Pallas kernels: 123 us -> 132 us  [project(): pl.pallas_call(project_kernel, in_specs=[pl.BlockSpec(memory_space=pl.ANY...]
    unnamed x3 -> x2, local copies, waits for them, and re-layouts: 3.79 us -> 5.11 us
where the time goes in v3:
time: 189 us
  Pallas kernels  180 us (95%)
  local copies, waits for them, and re-layouts  7.48 us (4%)
    pallas_call x1, Pallas kernels, project(): pl.pallas_call(project_kernel, in_specs=[pl.BlockSpec(memory_space=pl.ANY...  132 us
    pallas_call x1, Pallas kernels, mixer(): pl.pallas_call(mixer_kernel, in_specs=[pl.BlockSpec(memory_space=pltpu.SM...  48.6 us
    unnamed x2, local copies, waits for them, and re-layouts  5.11 us

profile of v3, /device:TPU:16, one launch (start us, length us, event | category | flops | bytes accessed | tf_op | source)
XLA Modules:
  0.0 188.5 jit_solution(7032845702320951184)
XLA Ops:
  0.6 1.9 %copy.16.w_out_ref = f32[1024,64]{1,0:T(8,128)} copy(f32[1024,64]{0,1:T(8,128)} %param.17) | data formatting | bytes 524288 | tf_op args[5]
  2.6 131.7 %project.1 = (bf16[3,512,1024]{2,1,0:T(8,128)(2,1)}, bf16[512,128]{1,0:T(8,128)(2,1)}, bf16[4,4,64,384]{3,2,1,0:T(8,128)(2,1)}, bf16[4,4,64,384]{3,2,1,0:T(8,128)(2,1)}, bf16[4,4,64,256]{3,2,1,0:T(8,128)(2,1)}) custom-call(bf16[512,4096]{1,0:T(8,128)(2,1)} %bitcast.12, s32[32,128]{1,0:T(8,128)} %bitcast.14, f32[1,4096]{1,0:T(1,128)} %bitcast.15, ...), custom_call_target="tpu_custom_call" | custom-call | flops 99999997952 | bytes 33554432 | tf_op jit(solution)/shard_map/project/pallas_call | solution.py:310
  134.3 48.6 %mixer.1 = (bf16[512,2048]{1,0:T(8,128)(2,1)}, f32[2,8,128,64]{3,2,1,0:T(8,128)}) custom-call(s32[2]{0:T(128)} %extents_ref.1, bf16[3,512,1024]{2,1,0:T(8,128)(2,1)} %get-tuple-element.9.rkv_ref, bf16[512,128]{1,0:T(8,128)(2,1)} %get-tuple-element.10.lora_ref, bf16[128,1024]{1,0:T(8,128)(2,1)} %right_ref.1, f32[1,1024]{1,0:T(1,128)} %bitcast.16, ...), custom_call_target="tpu_custom_call" | custom-call | flops 40000000000 | bytes 33554432 | tf_op jit(solution)/shard_map/mixer/pallas_call | solution.py:617
  183.0 2.4 %reshape.19 = f32[2,1,16,4096]{3,2,0,1:T(8,128)} reshape(f32[2,8,128,64]{3,2,1,0:T(8,128)} %get-tuple-element.15) | data formatting | bytes 1048576 | tf_op jit(solution)/shard_map/reshape | solution.py:685
  185.4 3.2 %copy.19 = bf16[2,256,2048]{2,1,0:T(8,128)(2,1)} copy(bf16[2,256,2048]{2,1,0:T(8,128)(2,1)} %bitcast.10) | data formatting | bytes 4194304

commit v4 on v3

--- a/solution.py
+++ b/solution.py
@@ -46,16 +46,6 @@
 
 def device(at):
     return (lax.axis_index("tensor"), at["x"] * SIDE + at["z"], at["y"])
-
-
-def greet_neighbours(at):
-    barrier = pltpu.get_barrier_semaphore()
-    for axis in "xyz":
-        for by in (1, -1):
-            pl.semaphore_signal(
-                barrier, inc=1, device_id=device(moved(at, axis, by)), device_id_type=MESH
-            )
-    pl.semaphore_wait(barrier, 6)
 
 
 class Ring:
@@ -115,11 +105,43 @@
             getattr(ring, name)(phase)
 
 
-def project_kernel(
-    x_ref, perm_ref, gain_ref, blend_ref, left_ref, w_ref, w_out_ref,
-    out_ref, lora_ref, plane0, plane1, plane2,
-    slots, slots0, slots1, slots2, stack, mixed, chosen, picked, total, stats, low_rank, last, tail,
-    load_sem, save_sem, tail_sem, send, recv, out_send, out_recv,
+def same_head():
+    c = lax.broadcasted_iota(jnp.int32, (PAIR, PAIR), 0) // ATTEND_DIM
+    v = lax.broadcasted_iota(jnp.int32, (PAIR, PAIR), 1) // ATTEND_DIM
+    return c == v
+
+
+LEVELS = 7
+QUAD = 256
+
+
+def windows():
+    t = lax.broadcasted_iota(jnp.int32, (CHUNK, QUAD), 0)
+    s = lax.broadcasted_iota(jnp.int32, (CHUNK, QUAD), 1) % CHUNK
+    chosen = [s < t, s > t]
+    for level in range(LEVELS):
+        middle = (((t >> (level + 1)) << 1) + 1) << level
+        late = ((s >= middle) & (s < t)) & (t >= middle)
+        early = ((s > t) & (s < middle)) & (t < middle)
+        chosen.append(late | early)
+    return [jnp.where(c, 1.0, 0.0).astype(bf16) for c in chosen]
+
+
+def halves(values):
+    first_head = lax.broadcasted_iota(jnp.int32, (1, PAIR), 1) < ATTEND_DIM
+    return jnp.concatenate(
+        [jnp.where(first_head, values, 0.0), jnp.where(first_head, 0.0, values)], axis=0
+    ).astype(bf16)
+
+
+def layer_kernel(
+    extents_ref, x_ref, perm_ref, gain_ref, blend_ref, left_ref, w_ref, w_out_ref,
+    right_ref, speed_ref, reward_ref, scale_ref,
+    out_ref, state_ref, slots0, slots1, slots2,
+    slots, stack, mixed, chosen, picked, total, stats, low_rank, lora_ref, last, tail, turned,
+    valid_ref, level_of, own_state, own_total, far_state, far_total,
+    load_sem, place_sem, tail_sem, send, recv, out_send, out_recv,
+    state_send, state_recv, total_send, total_recv, ready, fetch_sem, part_send, part_recv, save_sem,
 ):
     rows, width = x_ref.shape
     reqs = last.shape[0]
@@ -134,25 +156,38 @@
     load.start()
     for m in range(3):
         slots[(m, *(at[axis] for axis in PLACES[m]))] = w_ref[m].astype(bf16)
-    greet_neighbours(at)
+    core = lax.axis_index("tensor")
+    partner = (1 - core, lax.axis_index("req"), at["y"])
+    far_state[...] = jnp.zeros_like(far_state)
+    far_total[...] = jnp.zeros_like(far_total)
+    barrier = pltpu.get_barrier_semaphore()
+    friends = [device(moved(at, axis, by)) for axis in "xyz" for by in (1, -1)]
+    for friend in friends + [device(moved(at, "y", 2)), partner]:
+        pl.semaphore_signal(barrier, inc=1, device_id=friend, device_id_type=MESH)
+    pl.semaphore_wait(barrier, 8)
     each(rings, ("start", 0))
     load.wait()
     for b in range(reqs):
         end = (b + 1) * span
         last[b : b + 1, :] = stack[end - 16 : end, :].astype(f32)[15:16].astype(bf16)
-    hand_on = pltpu.make_async_remote_copy(
+    tail_on = pltpu.make_async_remote_copy(
         last, tail, tail_sem.at[0], tail_sem.at[1],
         device_id=device(moved(at, "y", 1)), device_id_type=MESH,
     )
-    hand_on.start()
+    tail_on.start()
 
     out_slots = (slots0, slots1, slots2)
     out_rings = []
-    turned = w_out_ref[...].T.astype(bf16)
+    turned[...] = w_out_ref[...].T.astype(bf16)
+    placed = []
     for i in range(3):
-        places = tuple(axis for axis in "xzy" if axis != ORDERS[i][2])
-        out_slots[i][tuple(at[axis] for axis in places)] = turned[:, OUT_CUTS[i] : OUT_CUTS[i + 1]]
-        out_rings.append(Ring(out_slots[i], ORDERS[i], places, out_send.at[i], out_recv.at[i], parts))
+        own = out_slots[i].at[at["x"], at["z"], at["y"]]
+        cut = turned.at[:, OUT_CUTS[i] : OUT_CUTS[i + 1]]
+        placed.append(pltpu.make_async_copy(cut, own, place_sem.at[i]))
+        placed[i].start()
+        out_rings.append(
+            Ring(out_slots[i], ORDERS[i], ("x", "z", "y"), out_send.at[i], out_recv.at[i], parts)
+        )
 
     table = jnp.concatenate([gain_ref[...], blend_ref[0:3, :]], axis=0)
     first = table.astype(bf16)
@@ -160,7 +195,7 @@
     second = rest.astype(bf16)
     third = (rest - second.astype(f32)).astype(bf16)
     each(rings, ("turn", 0))
-    hand_on.wait_recv()
+    tail_on.wait_recv()
     before = jnp.where(at["y"] > 0, tail[...].astype(f32), 0.0).astype(bf16)
     pad = jnp.zeros((16 - reqs - 12, width), bf16)
     stack[rows:, :] = jnp.concatenate([before, first, second, third, pad], axis=0)
@@ -178,6 +213,8 @@
 
     lax.fori_loop(0, stack.shape[0] // 16, row_stats, 0)
     each(rings, ("settle", 0), ("start", 1))
+    for place in placed:
+        place.wait()
 
     def shifted(values, gain):
         mean, scale = stats[0, :, 0:1], stats[1, :, 0:1]
@@ -273,7 +310,7 @@
             if fresh:
                 total[m, :, here] = product
             elif offset == 2:
-                out_ref[m, :, here] = (total[m, :, here] + product).astype(bf16)
+                mixed[m, own, :, here] = (total[m, :, here] + product).astype(bf16)
             else:
                 total[m, :, here] += product
             return 0
@@ -285,132 +322,8 @@
     products(1, False)
     products(3, False)
     each(out_rings, ("settle", 1))
-    saves = [
-        pltpu.make_async_copy(kept, plane, save_sem.at[i])
-        for i, (plane, kept) in enumerate(zip((plane0, plane1, plane2), out_slots))
-    ]
-    for save in saves:
-        save.start()
-    each(rings, ("far", 2))
-    products(2, False)
-    hand_on.wait_send()
-    for save in saves:
-        save.wait()
-    each(rings, ("sent", 0), ("sent", 1), ("sent", 2))
-    each(out_rings, ("sent", 0), ("sent", 1))
-
-
-def project(x, reqs, perm, gain, blend, left, weights, out_weight):
-    rows, width = x.shape
-    shard = weights.shape[1]
-    cuts = [OUT_CUTS[i + 1] - OUT_CUTS[i] for i in range(3)]
-    dma = pltpu.SemaphoreType.DMA
-    inner, local_width = left.shape[1], weights.shape[2]
-    vmem = pl.BlockSpec(memory_space=pltpu.VMEM)
-    return pl.pallas_call(
-        project_kernel,
-        in_specs=[pl.BlockSpec(memory_space=pl.ANY)] + [vmem] * 6,
-        out_specs=[vmem] * 2 + [pl.BlockSpec(memory_space=pl.ANY)] * 3,
-        out_shape=[
-            jax.ShapeDtypeStruct((3, rows, local_width), bf16),
-            jax.ShapeDtypeStruct((rows, inner), bf16),
-            *(jax.ShapeDtypeStruct((SIDE, SIDE, shard, cut), bf16) for cut in cuts),
-        ],
-        scratch_shapes=[
-            pltpu.VMEM((3, SIDE, SIDE, SIDE, *weights.shape[1:]), bf16),
-            *(pltpu.VMEM((SIDE, SIDE, shard, cut), bf16) for cut in cuts),
-            pltpu.VMEM((rows + 16, width), bf16),
-            pltpu.VMEM((3, SIDE, rows, width // SIDE), bf16),
-            pltpu.VMEM((width // 4, STEP), bf16),
-            pltpu.VMEM((rows + 16, STEP), f32),
-            pltpu.VMEM((3, rows, local_width), f32),
-            pltpu.VMEM((2, rows + 16, PAIR), f32),
-            pltpu.VMEM((rows, inner), f32),
-            pltpu.VMEM((reqs, width), bf16),
-            pltpu.VMEM((reqs, width), bf16),
-            dma, dma((3,)), dma((2,)),
-            dma((3, 3, 6)), dma((3, 3, 6)), dma((3, 2, 6)), dma((3, 2, 6)),
-        ],
-        compiler_params=pltpu.CompilerParams(
-            collective_id=0, has_side_effects=True, vmem_limit_bytes=61 << 20
-        ),
-        cost_estimate=pl.CostEstimate(
-            flops=100 * 10**9, bytes_accessed=32 << 20, transcendentals=0
-        ),
-        name="project",
-    )(x, perm, gain, blend, left, weights, out_weight)
-
-
-def same_head():
-    c = lax.broadcasted_iota(jnp.int32, (PAIR, PAIR), 0) // ATTEND_DIM
-    v = lax.broadcasted_iota(jnp.int32, (PAIR, PAIR), 1) // ATTEND_DIM
-    return c == v
-
-
-LEVELS = 7
-QUAD = 256
-
-
-def windows():
-    t = lax.broadcasted_iota(jnp.int32, (CHUNK, QUAD), 0)
-    s = lax.broadcasted_iota(jnp.int32, (CHUNK, QUAD), 1) % CHUNK
-    chosen = [s < t, s > t]
-    for level in range(LEVELS):
-        middle = (((t >> (level + 1)) << 1) + 1) << level
-        late = ((s >= middle) & (s < t)) & (t >= middle)
-        early = ((s > t) & (s < middle)) & (t < middle)
-        chosen.append(late | early)
-    return [jnp.where(c, 1.0, 0.0).astype(bf16) for c in chosen]
-
-
-def halves(values):
-    first_head = lax.broadcasted_iota(jnp.int32, (1, PAIR), 1) < ATTEND_DIM
-    return jnp.concatenate(
-        [jnp.where(first_head, values, 0.0), jnp.where(first_head, 0.0, values)], axis=0
-    ).astype(bf16)
-
-
-def mixer_kernel(
-    extents_ref, rkv_ref, lora_ref, right_ref, speed_ref, reward_ref, scale_ref, x_ref,
-    plane0, plane1, plane2,
-    out_ref, state_ref,
-    slots0, slots1, slots2, valid_ref, sums, level_of, decays, faded, y_buf, normed, expo,
-    own_state, own_total, far_state, far_total, outgoing, incoming, residual,
-    load_sem, plane_sem, send, recv, state_send, state_recv, total_send, total_recv, part_send, part_recv,
-):
-    rows, width = y_buf.shape
-    reqs = own_state.shape[0]
-    span = rows // reqs
-    at = position()
-    core = lax.axis_index("tensor")
-    partner = (1 - core, lax.axis_index("req"), at["y"])
-    share = x_ref.shape[1] // 2
-    load = pltpu.make_async_copy(
-        x_ref.at[:, pl.ds(pl.multiple_of(core * share, share), share)], residual, load_sem
-    )
-    load.start()
-    half = plane0.shape[2] // 2
-    parts = (slice(0, half), slice(half, 2 * half))
-    slots = (slots0, slots1, slots2)
-    rings = []
-    for i in range(3):
-        rings.append(Ring(slots[i], ORDERS[i], ("x", "z", "y"), send.at[i], recv.at[i], parts))
-    fills = []
-    for i, plane in enumerate((plane0, plane1, plane2)):
-        own = rings[i].block(2, at[ORDERS[i][2]], ())
-        fills.append(pltpu.make_async_copy(plane, own, plane_sem.at[i]))
-        fills[i].start()
-    far_state[...] = jnp.zeros_like(far_state)
-    far_total[...] = jnp.zeros_like(far_total)
-
-    barrier = pltpu.get_barrier_semaphore()
-    friends = [device(moved(at, axis, by)) for axis in "xyz" for by in (1, -1)]
-    for friend in friends + [device(moved(at, "y", 2)), partner]:
-        pl.semaphore_signal(barrier, inc=1, device_id=friend, device_id_type=MESH)
-    pl.semaphore_wait(barrier, 8)
-    for fill in fills:
-        fill.wait()
-    each(rings, ("start", 2))
+    sums = [(slice(CHUNK * i, CHUNK * (i + 1)), slice(0, QUAD)) for i in range(8)]
+    sums.append((slice(0, CHUNK), slice(QUAD, 2 * QUAD)))
     row = lax.broadcasted_iota(jnp.int32, (rows, PAIR), 0)
     token = at["y"] * span + row % span
     inside = jnp.zeros((rows, PAIR), f32)
@@ -419,13 +332,36 @@
     valid_ref[...] = inside
 
     for i, window in enumerate(windows()):
-        sums[i] = window
+        chosen[sums[i]] = window
     t = lax.broadcasted_iota(jnp.int32, (CHUNK, QUAD), 0)
     s = lax.broadcasted_iota(jnp.int32, (CHUNK, QUAD), 1) % CHUNK
     level = jnp.full((CHUNK, QUAD), LEVELS, jnp.int32)
     for i in range(LEVELS):
         level = jnp.where(((t >> i) == (s >> i) + 1) & (((t >> i) & 1) == 1), i, level)
     level_of[...] = level
+    each(rings, ("far", 2))
+    each(out_rings, ("start", 2))
+    products(2, False)
+    pl.semaphore_signal(ready, inc=1, device_id=partner, device_id_type=MESH)
+    def place(m, offset):
+        return mixed.at[m, (at[PLACES[m][0]] + offset) % SIDE]
+
+    rkv = [place(m, 0) for m in range(3)]
+    faded, normed = place(0, 1), place(0, 3)
+    y_buf, decays = total.at[0], total.at[1]
+    local_width = total.shape[2]
+    share = width // 2
+
+    def tiles(m, offsets):
+        planes = [(at[PLACES[m][0]] + offset) % SIDE for offset in offsets]
+
+        def tile(j):
+            plane = jnp.where(j < 4, planes[0], planes[1])
+            return mixed.at[m, plane, :, pl.ds(pl.multiple_of(j % 4 * QUAD, QUAD), QUAD)]
+
+        return tile
+
+    outgoing, incoming = tiles(1, (1, 2)), tiles(2, (1, 2))
     keep = same_head()
     ones = jnp.where(keep, 1.0, 0.0).astype(bf16)
     head_sum = jnp.concatenate([ones, ones], axis=0)
@@ -445,16 +381,16 @@
                 rows_c = slice(b * span + c * CHUNK, b * span + (c + 1) * CHUNK)
                 w = decays[rows_c, lanes]
                 both = jnp.concatenate(split_two(w), axis=0)
-                before.append(dot32(sums[0], both))
-                after.append(dot32(sums[1], both))
+                before.append(dot32(chosen[sums[0]], both))
+                after.append(dot32(chosen[sums[1]], both))
                 total.append(before[c][CHUNK - 1 :] + w[CHUNK - 1 :])
             own_total[b : b + 1, lanes] = total[0] + total[1]
             at0 = slice(b * span, b * span + CHUNK)
             at1 = slice(b * span + CHUNK, (b + 1) * span)
             whole = slice(b * span, (b + 1) * span)
-            r0, r1 = rkv_ref[0, at0, lanes].astype(f32), rkv_ref[0, at1, lanes].astype(f32)
-            k0 = rkv_ref[1, at0, lanes].astype(f32) * valid[at0]
-            k1 = rkv_ref[1, at1, lanes].astype(f32) * valid[at1]
+            r0, r1 = rkv[0][at0, lanes].astype(f32), rkv[0][at1, lanes].astype(f32)
+            k0 = rkv[1][at0, lanes].astype(f32) * valid[at0]
+            k1 = rkv[1][at1, lanes].astype(f32) * valid[at1]
             faded[at0, lanes] = (r0 * jnp.exp(before[0])).astype(bf16)
             faded[at1, lanes] = (r1 * jnp.exp(before[1] + total[0])).astype(bf16)
             query1 = (r1 * jnp.exp(before[1])).astype(bf16)
@@ -463,7 +399,7 @@
                 [(k0 * jnp.exp(after[0] + total[1])).astype(bf16), (k1 * jnp.exp(after[1])).astype(bf16)],
                 axis=0,
             )
-            value = rkv_ref[2, whole, lanes]
+            value = rkv[2][whole, lanes]
             bonus0 = r0 * k0 * reward_ref[:, lanes]
             bonus1 = r1 * k1 * reward_ref[:, lanes]
             for p in range(2):
@@ -482,7 +418,7 @@
 
         return 0
 
-    lax.fori_loop(0, width // QUAD, prepare, 0)
+    lax.fori_loop(0, local_width // QUAD, prepare, 0)
 
     def hand_on(by):
         to = device(moved(at, "y", by))
@@ -503,35 +439,40 @@
             for copy in hand_on(by):
                 copy.start()
 
+    def expo(n, p=None):
+        first = n % 2 * QUAD + (0 if p is None else p * PAIR)
+        lanes = slice(first, first + (QUAD if p is None else PAIR))
+        return slice(n // 2 * CHUNK, (n // 2 + 1) * CHUNK), lanes
+
     def within(i, _):
         q, c = i // 4, i % 4
         lanes = pl.ds(pl.multiple_of(q * QUAD, QUAD), QUAD)
         rows_c = pl.ds(pl.multiple_of(c * CHUNK, CHUNK), CHUNK)
         both = jnp.concatenate(split_two(decays[rows_c, lanes]), axis=0)
         for n in range(LEVELS):
-            expo[n] = dot32(sums[2 + n], both)
+            picked[expo(n)] = dot32(chosen[sums[2 + n]], both)
         row = lax.broadcasted_iota(jnp.int32, (CHUNK, 1), 0)
         valid = valid_ref[rows_c, 0:1]
         for p in range(2):
             pair = slice(p * PAIR, (p + 1) * PAIR)
             here = pl.ds(pl.multiple_of(q * QUAD + p * PAIR, PAIR), PAIR)
-            r = rkv_ref[0, rows_c, here].astype(f32)
-            k = rkv_ref[1, rows_c, here].astype(f32) * valid
+            r = rkv[0][rows_c, here].astype(f32)
+            k = rkv[1][rows_c, here].astype(f32) * valid
             scores = jnp.zeros((CHUNK, QUAD), f32)
             for n in range(LEVELS):
-                side = jnp.where(((row >> n) & 1) == 1, r, k) * jnp.exp(expo[n, :, pair])
+                side = jnp.where(((row >> n) & 1) == 1, r, k) * jnp.exp(picked[expo(n, p)])
                 found = dot32(side.astype(bf16), halves(side), CONTRACT_LANES)
                 scores = jnp.where(level_of[...] == n, found, scores)
-            values = halves(rkv_ref[2, rows_c, here].astype(f32))
+            values = halves(rkv[2][rows_c, here].astype(f32))
             y_buf[rows_c, here] += dot32(scores.astype(bf16), values)
 
         @pl.when(i == 3)
         def _():
-            each(rings, ("turn", 2))
-
-        return 0
-
-    lax.fori_loop(0, width // QUAD * (rows // CHUNK), within, 0)
+            each(out_rings, ("turn", 2))
+
+        return 0
+
+    lax.fori_loop(0, local_width // QUAD * (rows // CHUNK), within, 0)
 
     for by in range(1, SIDE):
         @pl.when(at["y"] >= by)
@@ -558,101 +499,130 @@
             normed[whole, here] = (scaled * valid_ref[whole, 0:1]).astype(bf16)
         return 0
 
-    lax.fori_loop(0, width // PAIR, finish, 0)
-    each(rings, ("settle", 2))
-
-    def terms(side, j):
-        product = None
-        for i in range(3):
-            weight = slots[i][2 * side + j // SIDE, j % SIDE]
-            weight = weight.reshape(SIDE * weight.shape[1], weight.shape[2])
-            part = dot32(normed[:, OUT_CUTS[i] : OUT_CUTS[i + 1]], weight, CONTRACT_LANES)
-            product = part if product is None else product + part
-        return product.astype(bf16)
+    lax.fori_loop(0, local_width // PAIR, finish, 0)
+    each(out_rings, ("settle", 2))
+
+    def fetch(t):
+        x, z = 2 * jnp.where(t < 8, 1 - core, core) + t % 8 // SIDE, t % SIDE
+        return [
+            pltpu.make_async_copy(
+                out_slots[i].at[x, z],
+                slots.at[0, x, z, :, :, OUT_CUTS[i] : OUT_CUTS[i + 1]],
+                fetch_sem.at[t, i],
+            )
+            for i in range(3)
+        ]
+
+    def begin(t, _):
+        for copy in fetch(t):
+            copy.start()
+        return 0
+
+    each(rings, ("sent", 0), ("sent", 1), ("sent", 2))
+    lax.fori_loop(0, 16, begin, 0)
+
+    def terms(t):
+        for copy in fetch(t):
+            copy.wait()
+        weight = slots[0, 2 * jnp.where(t < 8, 1 - core, core) + t % 8 // SIDE, t % SIDE]
+        weight = weight.reshape(QUAD, local_width)
+        return dot32(normed[...], weight, CONTRACT_LANES).astype(bf16)
 
     def exchange(j):
         return pltpu.make_async_remote_copy(
-            outgoing.at[j], incoming.at[j], part_send.at[j], part_recv.at[j],
+            outgoing(j), incoming(j), part_send.at[j], part_recv.at[j],
             device_id=partner, device_id_type=MESH,
         )
 
+    pl.semaphore_wait(ready, 1)
+
     def give(j, _):
-        outgoing[j] = terms(1 - core, j)
+        outgoing(j)[...] = terms(j)
         exchange(j).start()
         return 0
 
     lax.fori_loop(0, 8, give, 0)
-    load.wait()
+
+    def save(j):
+        here = pl.ds(pl.multiple_of(j * QUAD, QUAD), QUAD)
+        return pltpu.make_async_copy(incoming(j), out_ref.at[:, here], save_sem.at[j])
 
     def keep_own(j, _):
-        here = pl.ds(pl.multiple_of(j * QUAD, QUAD), QUAD)
-        mine = terms(core, j).astype(f32)
+        here = pl.ds(pl.multiple_of(core * share + j * QUAD, QUAD), QUAD)
+        mine = terms(j + 8).astype(f32)
         exchange(j).wait_recv()
-        summed = mine + incoming[j].astype(f32)
-        out_ref[:, here] = (residual[:, here].astype(f32) + summed).astype(bf16)
+        summed = mine + incoming(j)[...].astype(f32)
+        incoming(j)[...] = (stack[:rows, here].astype(f32) + summed).astype(bf16)
+        save(j).start()
         return 0
 
     lax.fori_loop(0, 8, keep_own, 0)
 
-    def sent(j, _):
+    def ended(j, _):
         exchange(j).wait_send()
-        return 0
-
-    lax.fori_loop(0, 8, sent, 0)
+        save(j).wait()
+        return 0
+
+    lax.fori_loop(0, 8, ended, 0)
     for by in range(1, SIDE):
         @pl.when(at["y"] + by < SIDE)
         def _():
             for copy in hand_on(by):
                 copy.wait_send()
-    each(rings, ("sent", 2))
-
-
-def mixer(extents, rkv, lora, right, speed, reward, scale, x, planes):
-    rows, width = rkv.shape[1:]
-    share, reqs, shard = x.shape[1] // 2, extents.shape[0], planes[0].shape[2]
-    pairs = width // PAIR
+    tail_on.wait_send()
+    each(out_rings, ("sent", 0), ("sent", 1), ("sent", 2))
+
+
+def layer(extents, x, perm, gain, blend, left, weights, out_weight, right, speed, reward, scale):
+    rows, width = x.shape
+    shard, local_width = weights.shape[1:]
+    reqs, inner, pairs = extents.shape[0], left.shape[1], local_width // PAIR
+    cuts = [OUT_CUTS[i + 1] - OUT_CUTS[i] for i in range(3)]
+    dma = pltpu.SemaphoreType.DMA
     vmem = pl.BlockSpec(memory_space=pltpu.VMEM)
     away = pl.BlockSpec(memory_space=pl.ANY)
-    dma = pltpu.SemaphoreType.DMA
-    return pl.pallas_call(
-        mixer_kernel,
-        in_specs=[pl.BlockSpec(memory_space=pltpu.SMEM)] + [vmem] * 6 + [away] * 4,
-        out_specs=[vmem, vmem],
+    hidden, final, *_ = pl.pallas_call(
+        layer_kernel,
+        in_specs=[pl.BlockSpec(memory_space=pltpu.SMEM), away] + [vmem] * 10,
+        out_specs=[away, vmem, away, away, away],
         out_shape=[
-            jax.ShapeDtypeStruct((rows, share), bf16),
+            jax.ShapeDtypeStruct((rows, width // 2), bf16),
             jax.ShapeDtypeStruct((reqs, pairs, PAIR, ATTEND_DIM), f32),
+            *(jax.ShapeDtypeStruct((SIDE, SIDE, SIDE, shard, cut), bf16) for cut in cuts),
         ],
         scratch_shapes=[
-            *(
-                pltpu.VMEM((SIDE, SIDE, SIDE, shard, OUT_CUTS[i + 1] - OUT_CUTS[i]), bf16)
-                for i in range(3)
-            ),
+            pltpu.VMEM((3, SIDE, SIDE, SIDE, shard, local_width), bf16),
+            pltpu.VMEM((rows + 16, width), bf16),
+            pltpu.VMEM((3, SIDE, rows, width // SIDE), bf16),
+            pltpu.VMEM((width // 4, STEP), bf16),
+            pltpu.VMEM((rows + 16, STEP), f32),
+            pltpu.VMEM((3, rows, local_width), f32),
+            pltpu.VMEM((2, rows + 16, PAIR), f32),
+            pltpu.VMEM((rows, inner), f32),
+            pltpu.VMEM((rows, inner), bf16),
+            pltpu.VMEM((reqs, width), bf16),
+            pltpu.VMEM((reqs, width), bf16),
+            pltpu.VMEM((shard, local_width), bf16),
             pltpu.VMEM((rows, PAIR), f32),
-            pltpu.VMEM((2 + LEVELS, CHUNK, QUAD), bf16),
             pltpu.VMEM((CHUNK, QUAD), jnp.int32),
-            pltpu.VMEM((rows, width), f32),
-            pltpu.VMEM((rows, width), bf16),
-            pltpu.VMEM((rows, width), f32),
-            pltpu.VMEM((rows, width), bf16),
-            pltpu.VMEM((LEVELS, CHUNK, QUAD), f32),
             pltpu.VMEM((reqs, pairs, ATTEND_DIM, PAIR), bf16),
-            pltpu.VMEM((reqs, width), f32),
+            pltpu.VMEM((reqs, local_width), f32),
             pltpu.VMEM((3, reqs, pairs, ATTEND_DIM, PAIR), bf16),
-            pltpu.VMEM((3, reqs, width), f32),
-            pltpu.VMEM((8, rows, QUAD), bf16),
-            pltpu.VMEM((8, rows, QUAD), bf16),
-            pltpu.VMEM((rows, share), bf16),
-            dma, dma((3,)),
-            dma((3, 3, 6)), dma((3, 3, 6)),
+            pltpu.VMEM((3, reqs, local_width), f32),
+            dma, dma((3,)), dma((2,)),
+            dma((3, 3, 6)), dma((3, 3, 6)), dma((3, 3, 6)), dma((3, 3, 6)),
             dma((3,)), dma((3,)), dma((3,)), dma((3,)),
-            dma((8,)), dma((8,)),
+            pltpu.SemaphoreType.REGULAR, dma((16, 3)), dma((8,)), dma((8,)), dma((8,)),
         ],
         compiler_params=pltpu.CompilerParams(
-            collective_id=1, has_side_effects=True, vmem_limit_bytes=56 << 20
+            collective_id=0, has_side_effects=True, vmem_limit_bytes=61 << 20
         ),
-        cost_estimate=pl.CostEstimate(flops=40 * 10**9, bytes_accessed=32 << 20, transcendentals=0),
-        name="mixer",
-    )(extents, rkv, lora, right, speed, reward, scale, x, *planes)
+        cost_estimate=pl.CostEstimate(
+            flops=100 * 10**9, bytes_accessed=64 << 20, transcendentals=0
+        ),
+        name="layer",
+    )(extents, x, perm, gain, blend, left, weights, out_weight, right, speed, reward, scale)
+    return hidden, final
 
 
 def local(
@@ -673,14 +643,11 @@
     rows = reqs * span
     local_width = feature_fading_speed.shape[0]
     x = incoming_activations.reshape(rows, width)
-    projected, lora, *planes = project(
-        x, reqs, learner_line_permutation.reshape(width // PAIR, PAIR), standardize_scaling[None],
-        lagged_blending_weights, fading_left_matrix, learner_acceptor_lookup_slices,
-        learner_projection_slices,
-    )
-    hidden, final = mixer(
-        prompt_extents, projected, lora, fading_right_matrix, feature_fading_speed[None],
-        self_reward[None], cluster_scaling_vector[None], x, planes,
+    hidden, final = layer(
+        prompt_extents, x, learner_line_permutation.reshape(width // PAIR, PAIR),
+        standardize_scaling[None], lagged_blending_weights, fading_left_matrix,
+        learner_acceptor_lookup_slices, learner_projection_slices, fading_right_matrix,
+        feature_fading_speed[None], self_reward[None], cluster_scaling_vector[None],
     )
     stretch_states = final.reshape(reqs, 1, local_width // ATTEND_DIM, ATTEND_DIM * ATTEND_DIM)
     return (hidden.reshape(reqs, span, hidden.shape[1]), stretch_states)

time: 189 us -> 186 us (0.984)
  Pallas kernels: 180 us -> 176 us
    pallas_call x2 -> x1, Pallas kernels: 180 us -> 176 us  [layer(): pl.pallas_call(layer_kernel, in_specs=[pl.BlockSpec(memory_space=pltpu.SM...]
where the time goes in v4:
time: 186 us; the launch traced here: 184 us
  Pallas kernels  176 us (95%)
  local copies, waits for them, and re-layouts  7.48 us (4%)
    pallas_call x1, Pallas kernels, layer(): pl.pallas_call(layer_kernel, in_specs=[pl.BlockSpec(memory_space=pltpu.SM...  176 us
    unnamed x2, local copies, waits for them, and re-layouts  5.11 us

profile of v4, /device:TPU:16, one launch (start us, length us, event | category | flops | bytes accessed | tf_op | source)
XLA Modules:
  0.0 183.8 jit_solution(4830210093937446196)
XLA Ops:
  0.6 1.9 %copy.16.w_out_ref = f32[1024,64]{1,0:T(8,128)} copy(f32[1024,64]{0,1:T(8,128)} %param.17) | data formatting | bytes 524288 | tf_op args[5]
  2.6 175.7 %layer.1 = (bf16[512,2048]{1,0:T(8,128)(2,1)}, f32[2,8,128,64]{3,2,1,0:T(8,128)}, bf16[4,4,4,64,384]{4,3,2,1,0:T(8,128)(2,1)}, bf16[4,4,4,64,384]{4,3,2,1,0:T(8,128)(2,1)}, bf16[4,4,4,64,256]{4,3,2,1,0:T(8,128)(2,1)}) custom-call(s32[2]{0:T(128)} %extents_ref.1, bf16[512,4096]{1,0:T(8,128)(2,1)} %bitcast.12, s32[32,128]{1,0:T(8,128)} %bitcast.13, ...), custom_call_target="tpu_custom_call" | custom-call | flops 99999997952 | bytes 67108864 | tf_op jit(solution)/shard_map/layer/pallas_call | solution.py:584
  178.3 2.4 %reshape.19 = f32[2,1,16,4096]{3,2,0,1:T(8,128)} reshape(f32[2,8,128,64]{3,2,1,0:T(8,128)} %get-tuple-element.5) | data formatting | bytes 1048576 | tf_op jit(solution)/shard_map/reshape | solution.py:652
  180.6 3.2 %copy.19 = bf16[2,256,2048]{2,1,0:T(8,128)(2,1)} copy(bf16[2,256,2048]{2,1,0:T(8,128)(2,1)} %bitcast.10) | data formatting | bytes 4194304

commit v5 on v4

--- a/solution.py
+++ b/solution.py
@@ -94,9 +94,17 @@
         self.near(phase)
         self.far(phase)
 
+    def own_sent(self, phase):
+        for slot in range(4):
+            self.copy(phase, slot).wait_send()
+
+    def passed_on(self, phase):
+        for slot in range(4, 6):
+            self.copy(phase, slot).wait_send()
+
     def sent(self, phase):
-        for slot in range(6):
-            self.copy(phase, slot).wait_send()
+        self.own_sent(phase)
+        self.passed_on(phase)
 
 
 def each(rings, *steps):
@@ -178,7 +186,7 @@
 
     out_slots = (slots0, slots1, slots2)
     out_rings = []
-    turned[...] = w_out_ref[...].T.astype(bf16)
+    turned[...] = w_out_ref[...].astype(bf16)
     placed = []
     for i in range(3):
         own = out_slots[i].at[at["x"], at["z"], at["y"]]
@@ -339,17 +347,50 @@
     for i in range(LEVELS):
         level = jnp.where(((t >> i) == (s >> i) + 1) & (((t >> i) & 1) == 1), i, level)
     level_of[...] = level
+    local_width = total.shape[2]
+
+    def place(m, offset):
+        return mixed.at[m, (at[PLACES[m][0]] + offset) % SIDE]
+
+    high_decay, low_decay = place(1, 3), place(2, 3)
+
+    def decay(q, _):
+        lanes = pl.ds(pl.multiple_of(q * QUAD, QUAD), QUAD)
+        rate = jnp.exp(dot32(lora_ref[...], right_ref[:, lanes]))
+        high, low = split_two(-speed_ref[:, lanes] * rate * valid_ref[:, 0:1])
+        high_decay[:, lanes], low_decay[:, lanes] = high, low
+        return 0
+
+    lax.fori_loop(0, local_width // QUAD, decay, 0)
+
+    def split_decay(rows_c, lanes):
+        return jnp.concatenate([high_decay[rows_c, lanes], low_decay[rows_c, lanes]], axis=0)
+
+    each(rings, ("sent", 0), ("sent", 1), ("own_sent", 2))
+
+    def level_decay(n, c, lanes):
+        m, part = (n - 1) // 2, (n - 1) % 2
+        return (
+            m, at[PLACES[m][0]], 2 * part + c // 2, pl.ds(c % 2 * 2, 2), slice(None), lanes
+        )
+
+    def fade(i, _):
+        q, c = i // 4, i % 4
+        lanes = pl.ds(pl.multiple_of(q * QUAD, QUAD), QUAD)
+        both = split_decay(pl.ds(pl.multiple_of(c * CHUNK, CHUNK), CHUNK), lanes)
+        for n in range(1, LEVELS):
+            faint = jnp.exp(dot32(chosen[sums[2 + n]], both)).astype(bf16)
+            slots[level_decay(n, c, lanes)] = faint.reshape(2, CHUNK // 2, QUAD)
+        return 0
+
+    lax.fori_loop(0, local_width // QUAD * (rows // CHUNK), fade, 0)
     each(rings, ("far", 2))
     each(out_rings, ("start", 2))
     products(2, False)
     pl.semaphore_signal(ready, inc=1, device_id=partner, device_id_type=MESH)
-    def place(m, offset):
-        return mixed.at[m, (at[PLACES[m][0]] + offset) % SIDE]
-
     rkv = [place(m, 0) for m in range(3)]
     faded, normed = place(0, 1), place(0, 3)
-    y_buf, decays = total.at[0], total.at[1]
-    local_width = total.shape[2]
+    y_buf = total.at[0]
     share = width // 2
 
     def tiles(m, offsets):
@@ -373,14 +414,12 @@
     def prepare(q, _):
         lanes = pl.ds(pl.multiple_of(q * QUAD, QUAD), QUAD)
         valid = valid_ref[:, 0:1]
-        rate = jnp.exp(dot32(lora_ref[...], right_ref[:, lanes]))
-        decays[:, lanes] = -speed_ref[:, lanes] * rate * valid
         for b in range(reqs):
             before, after, total = [], [], []
             for c in range(span // CHUNK):
                 rows_c = slice(b * span + c * CHUNK, b * span + (c + 1) * CHUNK)
-                w = decays[rows_c, lanes]
-                both = jnp.concatenate(split_two(w), axis=0)
+                both = split_decay(rows_c, lanes)
+                w = both[:CHUNK].astype(f32) + both[CHUNK:].astype(f32)
                 before.append(dot32(chosen[sums[0]], both))
                 after.append(dot32(chosen[sums[1]], both))
                 total.append(before[c][CHUNK - 1 :] + w[CHUNK - 1 :])
@@ -439,18 +478,9 @@
             for copy in hand_on(by):
                 copy.start()
 
-    def expo(n, p=None):
-        first = n % 2 * QUAD + (0 if p is None else p * PAIR)
-        lanes = slice(first, first + (QUAD if p is None else PAIR))
-        return slice(n // 2 * CHUNK, (n // 2 + 1) * CHUNK), lanes
-
     def within(i, _):
         q, c = i // 4, i % 4
-        lanes = pl.ds(pl.multiple_of(q * QUAD, QUAD), QUAD)
         rows_c = pl.ds(pl.multiple_of(c * CHUNK, CHUNK), CHUNK)
-        both = jnp.concatenate(split_two(decays[rows_c, lanes]), axis=0)
-        for n in range(LEVELS):
-            picked[expo(n)] = dot32(chosen[sums[2 + n]], both)
         row = lax.broadcasted_iota(jnp.int32, (CHUNK, 1), 0)
         valid = valid_ref[rows_c, 0:1]
         for p in range(2):
@@ -460,7 +490,9 @@
             k = rkv[1][rows_c, here].astype(f32) * valid
             scores = jnp.zeros((CHUNK, QUAD), f32)
             for n in range(LEVELS):
-                side = jnp.where(((row >> n) & 1) == 1, r, k) * jnp.exp(picked[expo(n, p)])
+                side = jnp.where(((row >> n) & 1) == 1, r, k)
+                if n > 0:
+                    side = side * slots[level_decay(n, c, here)].reshape(CHUNK, PAIR).astype(f32)
                 found = dot32(side.astype(bf16), halves(side), CONTRACT_LANES)
                 scores = jnp.where(level_of[...] == n, found, scores)
             values = halves(rkv[2][rows_c, here].astype(f32))
@@ -474,6 +506,21 @@
 
     lax.fori_loop(0, local_width // QUAD * (rows // CHUNK), within, 0)
 
+    def fetch(i, offset):
+        axis = ORDERS[i][2]
+        index = [slice(None)] * 3
+        index["xzy".index(axis)] = (at[axis] + offset) % SIDE
+        cut = slice(OUT_CUTS[i], OUT_CUTS[i + 1])
+        return pltpu.make_async_copy(
+            out_slots[i].at[tuple(index)], slots.at[(0, *index, slice(None), cut)],
+            fetch_sem.at[i, offset],
+        )
+
+    each(rings, ("passed_on", 2))
+    each(out_rings, ("near", 2))
+    for i in range(3):
+        for offset in (0, 1, 3):
+            fetch(i, offset).start()
     for by in range(1, SIDE):
         @pl.when(at["y"] >= by)
         def _():
@@ -500,30 +547,14 @@
         return 0
 
     lax.fori_loop(0, local_width // PAIR, finish, 0)
-    each(out_rings, ("settle", 2))
-
-    def fetch(t):
-        x, z = 2 * jnp.where(t < 8, 1 - core, core) + t % 8 // SIDE, t % SIDE
-        return [
-            pltpu.make_async_copy(
-                out_slots[i].at[x, z],
-                slots.at[0, x, z, :, :, OUT_CUTS[i] : OUT_CUTS[i + 1]],
-                fetch_sem.at[t, i],
-            )
-            for i in range(3)
-        ]
-
-    def begin(t, _):
-        for copy in fetch(t):
-            copy.start()
-        return 0
-
-    each(rings, ("sent", 0), ("sent", 1), ("sent", 2))
-    lax.fori_loop(0, 16, begin, 0)
+    each(out_rings, ("far", 2))
+    for i in range(3):
+        fetch(i, 2).start()
+    for i in range(3):
+        for offset in range(SIDE):
+            fetch(i, offset).wait()
 
     def terms(t):
-        for copy in fetch(t):
-            copy.wait()
         weight = slots[0, 2 * jnp.where(t < 8, 1 - core, core) + t % 8 // SIDE, t % SIDE]
         weight = weight.reshape(QUAD, local_width)
         return dot32(normed[...], weight, CONTRACT_LANES).astype(bf16)
@@ -612,7 +643,7 @@
             dma, dma((3,)), dma((2,)),
             dma((3, 3, 6)), dma((3, 3, 6)), dma((3, 3, 6)), dma((3, 3, 6)),
             dma((3,)), dma((3,)), dma((3,)), dma((3,)),
-            pltpu.SemaphoreType.REGULAR, dma((16, 3)), dma((8,)), dma((8,)), dma((8,)),
+            pltpu.SemaphoreType.REGULAR, dma((3, SIDE)), dma((8,)), dma((8,)), dma((8,)),
         ],
         compiler_params=pltpu.CompilerParams(
             collective_id=0, has_side_effects=True, vmem_limit_bytes=61 << 20
@@ -646,7 +677,7 @@
     hidden, final = layer(
         prompt_extents, x, learner_line_permutation.reshape(width // PAIR, PAIR),
         standardize_scaling[None], lagged_blending_weights, fading_left_matrix,
-        learner_acceptor_lookup_slices, learner_projection_slices, fading_right_matrix,
+        learner_acceptor_lookup_slices, learner_projection_slices.T, fading_right_matrix,
         feature_fading_speed[None], self_reward[None], cluster_scaling_vector[None],
     )
     stretch_states = final.reshape(reqs, 1, local_width // ATTEND_DIM, ATTEND_DIM * ATTEND_DIM)

time: 186 us -> 178 us (0.957); the launches traced: 184 us -> 178 us
  Pallas kernels: 176 us -> 172 us
  local copies, waits for them, and re-layouts: 7.48 us -> 5.53 us
    pallas_call x1, Pallas kernels: 176 us -> 172 us  [layer(): pl.pallas_call(layer_kernel, in_specs=[pl.BlockSpec(memory_space=pltpu.SM...]
    unnamed x2 -> x1, local copies, waits for them, and re-layouts: 5.11 us -> 3.16 us
where the time goes in v5:
time: 178 us
  Pallas kernels  172 us (97%)
  local copies, waits for them, and re-layouts  5.53 us (3%)
    pallas_call x1, Pallas kernels, layer(): pl.pallas_call(layer_kernel, in_specs=[pl.BlockSpec(memory_space=pltpu.SM...  172 us

profile of v5, /device:TPU:16, one launch (start us, length us, event | category | flops | bytes accessed | tf_op | source)
XLA Modules:
  0.0 177.9 jit_solution(17637146221531618799)
XLA Ops:
  0.6 171.8 %layer.1 = (bf16[512,2048]{1,0:T(8,128)(2,1)}, f32[2,8,128,64]{3,2,1,0:T(8,128)}, bf16[4,4,4,64,384]{4,3,2,1,0:T(8,128)(2,1)}, bf16[4,4,4,64,384]{4,3,2,1,0:T(8,128)(2,1)}, bf16[4,4,4,64,256]{4,3,2,1,0:T(8,128)(2,1)}) custom-call(s32[2]{0:T(128)} %extents_ref.1, bf16[512,4096]{1,0:T(8,128)(2,1)} %bitcast.13, s32[32,128]{1,0:T(8,128)} %bitcast.15, ...), custom_call_target="tpu_custom_call" | custom-call | flops 99999997952 | bytes 67108864 | tf_op jit(solution)/shard_map/layer/pallas_call | solution.py:615
  172.4 2.4 %reshape.19 = f32[2,1,16,4096]{3,2,0,1:T(8,128)} reshape(f32[2,8,128,64]{3,2,1,0:T(8,128)} %get-tuple-element.5) | data formatting | bytes 1048576 | tf_op jit(solution)/shard_map/reshape | solution.py:683
  174.8 3.2 %copy.17 = bf16[2,256,2048]{2,1,0:T(8,128)(2,1)} copy(bf16[2,256,2048]{2,1,0:T(8,128)(2,1)} %bitcast.11) | data formatting | bytes 4194304

commit v6 on v5

--- a/solution.py
+++ b/solution.py
@@ -307,7 +307,7 @@
     lax.fori_loop(0, width // STEP, mix_step, 0)
     lora_ref[...] = jnp.tanh(low_rank[...]).astype(bf16)
 
-    def products(offset, fresh):
+    def products(offset, fresh, tiles=(0, 12)):
         def tile(i, _):
             m, n = i // 4, i % 4
             own = jnp.where(m == 0, at["z"], jnp.where(m == 1, at["x"], at["y"]))
@@ -323,7 +323,7 @@
                 total[m, :, here] += product
             return 0
 
-        lax.fori_loop(0, 12, tile, 0)
+        lax.fori_loop(*tiles, tile, 0)
 
     products(0, True)
     each(rings, ("near", 2))
@@ -384,9 +384,10 @@
         return 0
 
     lax.fori_loop(0, local_width // QUAD * (rows // CHUNK), fade, 0)
-    each(rings, ("far", 2))
     each(out_rings, ("start", 2))
-    products(2, False)
+    for m in range(3):
+        rings[m].far(2)
+        products(2, False, (4 * m, 4 * m + 4))
     pl.semaphore_signal(ready, inc=1, device_id=partner, device_id_type=MESH)
     rkv = [place(m, 0) for m in range(3)]
     faded, normed = place(0, 1), place(0, 3)

time: 178 us -> 178 us (level)
  no operation moved by 1% of the time
where the time goes in v6:
time: 178 us
  Pallas kernels  172 us (97%)
  local copies, waits for them, and re-layouts  5.53 us (3%)
    pallas_call x1, Pallas kernels, layer(): pl.pallas_call(layer_kernel, in_specs=[pl.BlockSpec(memory_space=pltpu.SM...  172 us

profile of v6, /device:TPU:16, one launch (start us, length us, event | category | flops | bytes accessed | tf_op | source)
XLA Modules:
  0.0 177.9 jit_solution(300437833715980128)
XLA Ops:
  0.6 171.8 %layer.1 = (bf16[512,2048]{1,0:T(8,128)(2,1)}, f32[2,8,128,64]{3,2,1,0:T(8,128)}, bf16[4,4,4,64,384]{4,3,2,1,0:T(8,128)(2,1)}, bf16[4,4,4,64,384]{4,3,2,1,0:T(8,128)(2,1)}, bf16[4,4,4,64,256]{4,3,2,1,0:T(8,128)(2,1)}) custom-call(s32[2]{0:T(128)} %extents_ref.1, bf16[512,4096]{1,0:T(8,128)(2,1)} %bitcast.13, s32[32,128]{1,0:T(8,128)} %bitcast.15, ...), custom_call_target="tpu_custom_call" | custom-call | flops 99999997952 | bytes 67108864 | tf_op jit(solution)/shard_map/layer/pallas_call | solution.py:616
  172.4 2.4 %reshape.19 = f32[2,1,16,4096]{3,2,0,1:T(8,128)} reshape(f32[2,8,128,64]{3,2,1,0:T(8,128)} %get-tuple-element.5) | data formatting | bytes 1048576 | tf_op jit(solution)/shard_map/reshape | solution.py:684
  174.8 3.2 %copy.17 = bf16[2,256,2048]{2,1,0:T(8,128)(2,1)} copy(bf16[2,256,2048]{2,1,0:T(8,128)(2,1)} %bitcast.11) | data formatting | bytes 4194304
